TPU v7x, 32 devices: a whole 2x2x4 slice. The times are simulated.
32 devices in a mesh: row: 16 (over z, x, core), col: 2 (over y).
Axes of the slice: x: 2, y: 2, z: 4, core: 2. Of those that a mesh axis runs over, the one named last changes fastest.
Arguments:
- ham: bfloat16 [8192, 8192], P('row'), may hold values from -0.2 to 1.7, as said below
- coeff: bfloat16 [8192, 8192], P('row', 'col'), may hold values from -40 to 40, as said below
- tile_mask: int32 [256, 256], P('row'), may hold values from 0 to 1, as said below
- occupation: int32 [16, 8192], replicated, may hold values from 0 to 1, as said below
- orbital_energy: float32 [16], replicated, may hold values from -0.4 to 0.6
- coulomb: float32 [16, 16], replicated, may hold values from 0.005 to 0.04
Outputs:
- correction: float32 [8192, 8192], P('row', 'col')
- stats: float32 [2], replicated
Inputs may be any that keep to these rules, and one draw needn't show every extreme that they name: ham is symmetric. coeff is symmetric. tile_mask is symmetric with ones on its diagonal. `occupation`: every column holds exactly 6 ones.
All inputs are finite; a program needn't handle non-finite values.
Results may differ from a plain program's by a relative error of at most 0.0003.
Values may be sent and summed in bfloat16 or wider, within the bound.
A program may use at most 192 MiB of HBM per device.

v0:
```python
import functools
import math

import jax
import jax.numpy as jnp
from jax import lax
from jax.experimental import pallas as pl
from jax.experimental.layout import Layout, with_layout_constraint
from jax.experimental.pallas import tpu as pltpu
from jax.sharding import PartitionSpec as P

MESH = pl.DeviceIdType.MESH
HIGH = lax.Precision.HIGHEST


def turn_kernel(row_count, col_count, total, chunk, chunks, *refs):
    last = chunk == chunks - 1
    if last:
        products, arrived = refs[:chunks], refs[chunks : 2 * chunks - 1]
        diagonal_ref, c_ref, out_ref, stats_ref, recv = refs[2 * chunks - 1 : 2 * chunks + 4]
        refs = refs[2 * chunks + 4 :]
        mine, sums, sum_send, sum_recv = refs[-4:]
    else:
        products = refs[:1]
        recv = refs[1]
        refs = refs[2:]
    p_ref, packed, relay_a, relay_b, load_sem, own_send, recv_sem, arrive_a, arrive_b, send_a, send_b, self_sem = refs[:12]
    row = lax.axis_index("row")
    col = lax.axis_index("col")
    tile = p_ref.shape[0]
    half = tile // 2
    fold = row_count // col_count
    per = fold // chunks
    home = lax.div(row, fold)
    place = lax.rem(row, fold)
    turn = lax.div(place, chunks)
    count = row_count * col_count
    me = row * col_count + col
    is_home = home == col
    takes = lax.rem(place, chunks) == chunk
    if last:
        loads = [
            pltpu.make_async_copy(
                product.at[:, pl.ds(k * tile, tile)],
                p_ref.at[:, pl.ds((q + chunks * k) * tile, tile)],
                load_sem.at[q * per + k],
            )
            for q, product in enumerate(products)
            for k in range(per)
        ]
    else:
        loads = [pltpu.make_async_copy(products[0], p_ref, load_sem.at[0])]
    for load in loads:
        load.start()
    if last:
        diagonal_load = pltpu.make_async_copy(diagonal_ref, out_ref, self_sem.at[3])
        diagonal_load.start()

    barrier = pltpu.get_barrier_semaphore()

    def greet(d, carry):
        other = lax.rem(me + d, count)
        pl.semaphore_signal(
            barrier,
            inc=1,
            device_id=(lax.div(other, col_count), lax.rem(other, col_count)),
            device_id_type=MESH,
        )
        return carry

    lax.fori_loop(1, count, greet, 0)
    pl.semaphore_wait(barrier, count - 1)
    for load in loads:
        load.wait()

    def columns(s):
        return pl.ds(pl.multiple_of(s * tile, tile), tile)

    def remote(src, dst, send, arrive, to_row, to_col):
        return pltpu.make_async_remote_copy(
            src_ref=src,
            dst_ref=dst,
            send_sem=send,
            recv_sem=arrive,
            device_id=(to_row, to_col),
            device_id_type=MESH,
        )

    def spot(k):
        kk = lax.rem(turn + k, per)
        return kk, chunk + chunks * kk

    def own_direct(k):
        kk, s = spot(k)
        near = col * fold + s
        return [
            remote(packed.at[kk, h], recv.at[place, h], own_send.at[kk, h], recv_sem.at[place, h], near, col)
            for h in range(2)
        ]

    def own_relayed(k):
        kk, s = spot(k)
        near = col * fold + s
        slot_a = col - (col > home).astype(jnp.int32)
        slot_b = row - fold * (home > col).astype(jnp.int32)
        return [
            remote(packed.at[kk, 0], relay_a.at[slot_a, kk], own_send.at[kk, 0], arrive_a.at[slot_a, kk], row, home),
            remote(packed.at[kk, 1], relay_b.at[slot_b], own_send.at[kk, 1], arrive_b.at[slot_b], near, col),
        ]

    def own_local():
        return [pltpu.make_async_copy(packed.at[turn, h], recv.at[place, h], self_sem.at[h]) for h in range(2)]

    def pack(k):
        kk, s = spot(k)
        cols = columns(s) if last else columns(kk)
        for h in range(2):
            peak = jnp.max(jnp.abs(p_ref[pl.ds(h * half, half), cols]), axis=0, keepdims=True)
            code = jnp.floor(jnp.log2(jnp.maximum(peak, 1e-30)) * 128.0) + 2.0
            grow = jnp.exp2(code * (-1.0 / 128.0)) * 32767.0
            packed[kk, h, pl.ds(half, 16)] = jnp.broadcast_to(code, (16, tile)).astype(jnp.int32).astype(jnp.int16)
            rows = min(64, half)
            for r in range(0, half, rows):
                value = p_ref[pl.ds(h * half + r, rows), cols] * grow
                packed[kk, h, pl.ds(r, rows)] = jnp.floor(value + 0.5).astype(jnp.int32).astype(jnp.int16)

    def exchange(phase, start):
        def one(d, carry):
            other = lax.rem(me + d, count)
            copy = remote(
                mine.at[phase],
                sums.at[phase, me],
                sum_send.at[phase, d],
                sum_recv.at[phase, me],
                lax.div(other, col_count),
                lax.rem(other, col_count),
            )
            if start:
                copy.start()
            else:
                copy.wait_send()
            return carry

        lax.fori_loop(1, count, one, 0)

    def gather_sums(phase):
        def one(d, carry):
            other = lax.rem(me + d, count)
            remote(
                mine.at[phase],
                sums.at[phase, other],
                sum_send.at[phase, d],
                sum_recv.at[phase, other],
                lax.div(other, col_count),
                lax.rem(other, col_count),
            ).wait_recv()
            return carry

        lax.fori_loop(1, count, one, 0)
        sums[phase, pl.ds(me, 1)] = mine[pl.ds(phase, 1)]
        every = jnp.sum(sums[phase], axis=0)
        return jnp.sum(every[0:8]), jnp.sum(every[8:16])

    def fold_sum(x):
        lanes = x.shape[1] // 128
        out = x[:, 0:128]
        for q in range(1, lanes):
            out = out + x[:, q * 128 : (q + 1) * 128]
        return jnp.sum(out.reshape(x.shape[0] // 8, 8, 128), axis=0)

    zero = jnp.zeros((8, 128), jnp.float32)
    if last:
        step_rows = min(32, tile)

        def early(r, carry):
            rows = pl.ds(pl.multiple_of(r * step_rows, step_rows), step_rows)
            c = c_ref[rows, :].astype(jnp.float32)
            return carry[0] + fold_sum(c * p_ref[rows, :]), carry[1] + fold_sum(c * c)

        proj, weight = lax.fori_loop(0, tile // step_rows, early, (zero, zero))
        mine[0, 0:8] = proj
        mine[0, 8:16] = weight
        exchange(0, True)

    def launch(k, carry):
        pack(k)

        @pl.when(jnp.logical_not(is_home))
        def _():
            for copy in own_relayed(k):
                copy.start()

        @pl.when(jnp.logical_and(is_home, jnp.logical_or(k > 0, jnp.logical_not(takes))))
        def _():
            for copy in own_direct(k):
                copy.start()

        return carry

    lax.fori_loop(0, per, launch, 0)

    @pl.when(jnp.logical_and(is_home, takes))
    def _():
        for copy in own_local():
            copy.start()
        for copy in own_local():
            copy.wait()

    def relay_first(t):
        slot = lax.div(t, per)
        group = slot + (slot >= col).astype(jnp.int32)
        kk, s = spot(lax.rem(t, per))
        return slot, kk, remote(
            relay_a.at[slot, kk], recv.at[place, 0], send_a.at[t], recv_sem.at[place, 0], group * fold + s, col
        )

    def relay_second(t):
        slot = lax.div(t, fold)
        group = slot + (slot >= col).astype(jnp.int32)
        far = lax.rem(place - lax.rem(t, fold) + fold, fold)
        slot_b = slot * fold + far
        return slot_b, remote(
            relay_b.at[slot_b], recv.at[far, 1], send_b.at[t], recv_sem.at[far, 1], row, group
        )

    @pl.when(is_home)
    def _():
        def step(t, carry):
            slot, kk, copy = relay_first(t)
            pltpu.make_async_copy(relay_a.at[slot, kk], relay_a.at[slot, kk], arrive_a.at[slot, kk]).wait()
            copy.start()
            return carry

        lax.fori_loop(0, (col_count - 1) * per, step, 0)

    @pl.when(jnp.logical_and(is_home, takes))
    def _():
        def step(t, carry):
            slot_b, copy = relay_second(t)
            pltpu.make_async_copy(relay_b.at[slot_b], relay_b.at[slot_b], arrive_b.at[slot_b]).wait()
            copy.start()
            return carry

        lax.fori_loop(0, (col_count - 1) * fold, step, 0)

    def await_piece(k):
        s = lax.rem(place - k + fold, fold)

        @pl.when(jnp.logical_and(takes, jnp.logical_not(jnp.logical_and(is_home, k == 0))))
        def _():
            for h in range(2):
                pltpu.make_async_copy(recv.at[s, h], recv.at[s, h], recv_sem.at[s, h]).wait()

    def settle():
        @pl.when(is_home)
        def _():
            def done(k, carry):
                @pl.when(jnp.logical_or(k > 0, jnp.logical_not(takes)))
                def _():
                    for copy in own_direct(k):
                        copy.wait_send()

                return carry

            lax.fori_loop(0, per, done, 0)

            def done_first(t, carry):
                relay_first(t)[-1].wait_send()
                return carry

            lax.fori_loop(0, (col_count - 1) * per, done_first, 0)

        @pl.when(jnp.logical_and(is_home, takes))
        def _():
            def done_second(t, carry):
                relay_second(t)[-1].wait_send()
                return carry

            lax.fori_loop(0, (col_count - 1) * fold, done_second, 0)

        @pl.when(jnp.logical_not(is_home))
        def _():
            def done(k, carry):
                for copy in own_relayed(k):
                    copy.wait_send()
                return carry

            lax.fori_loop(0, per, done, 0)

    if not last:

        def hold(k, carry):
            await_piece(k)
            return carry

        lax.fori_loop(0, fold, hold, 0)
        settle()
        return

    for q, ready in enumerate(arrived):

        @pl.when(lax.rem(place, chunks) == q)
        def _():
            fetch = pltpu.make_async_copy(ready, recv, self_sem.at[2])
            fetch.start()
            fetch.wait()

    proj, weight = gather_sums(0)
    theta = 2.0 * proj / weight
    diagonal_load.wait()

    piece = min(128, tile)

    def finish(k, carry):
        s = lax.rem(place - k + fold, fold)

        await_piece(k)

        def part(r, carry):
            squares, spread = carry
            rows = pl.ds(pl.multiple_of(r * piece, piece), piece)
            for h in range(2):
                cols = pl.ds(pl.multiple_of(s * tile + h * half, half), half)
                code = recv[s, h, pl.ds(half, 16), rows].astype(jnp.int32).astype(jnp.float32)[0:1]
                shrink = jnp.exp2(code * (1.0 / 128.0)) * (1.0 / 32767.0)
                value = recv[s, h, pl.ds(0, half), rows].astype(jnp.int32).astype(jnp.float32)
                turned = (value * shrink).T
                sigma = p_ref[rows, cols] + turned
                residual = sigma - theta * c_ref[rows, cols].astype(jnp.float32)
                update = residual / jnp.maximum(jnp.abs(out_ref[rows, cols] - theta), 1.0)
                out_ref[rows, cols] = update
                squares = squares + fold_sum(residual * residual)
                spread = spread + fold_sum(update * update)
            return squares, spread

        return lax.fori_loop(0, tile // piece, part, carry)

    squares, spread = lax.fori_loop(0, fold, finish, (zero, zero))
    mine[1, 0:8] = squares
    mine[1, 8:16] = spread
    exchange(1, True)
    squares, spread = gather_sums(1)
    stats_ref[0] = theta
    stats_ref[1] = squares / total
    stats_ref[2] = spread / total

    exchange(0, False)
    exchange(1, False)
    settle()


def turn(chunk, chunks, products, arrived, coeff, diagonal, strings):
    tile_rows, tile_cols = coeff.shape
    row_count = lax.axis_size("row")
    col_count = lax.axis_size("col")
    fold = row_count // col_count
    per = fold // chunks
    count = row_count * col_count
    tall = tile_rows // 2 + 16
    others = max(col_count - 1, 1)
    vmem = pl.BlockSpec(memory_space=pltpu.VMEM)
    anywhere = pl.BlockSpec(memory_space=pl.ANY)
    dma = pltpu.SemaphoreType.DMA
    last = chunk == chunks - 1
    arrival = (fold, 2, tall, tile_rows)
    scratch = [
        pltpu.VMEM((tile_rows, tile_cols if last else tile_cols // chunks), jnp.float32),
        pltpu.VMEM((per, 2, tall, tile_rows), jnp.int16),
        pltpu.VMEM((others, per, tall, tile_rows), jnp.int16),
        pltpu.VMEM((others * fold, tall, tile_rows), jnp.int16),
        dma((fold,)),
        dma((per, 2)),
        dma((fold, 2)),
        dma((others, per)),
        dma((others * fold,)),
        dma((others * per,)),
        dma((others * fold,)),
        dma((4,)),
    ]
    if last:
        operands = (*products, *arrived, diagonal, coeff)
        in_specs = [anywhere] * (2 * chunks) + [vmem]
        out_shape = (
            jax.ShapeDtypeStruct((tile_rows, tile_cols), jnp.float32),
            jax.ShapeDtypeStruct((3,), jnp.float32),
        )
        out_specs = (vmem, pl.BlockSpec(memory_space=pltpu.SMEM))
        scratch = [
            pltpu.VMEM(arrival, jnp.int16),
            *scratch,
            pltpu.VMEM((2, 16, 128), jnp.float32),
            pltpu.VMEM((2, count, 16, 128), jnp.float32),
            dma((2, count)),
            dma((2, count)),
        ]
    else:
        operands = (products[chunk],)
        in_specs = [anywhere]
        out_shape = jax.ShapeDtypeStruct(arrival, jnp.int16)
        out_specs = vmem
    return pl.pallas_call(
        functools.partial(turn_kernel, row_count, col_count, float(strings) * float(strings), chunk, chunks),
        out_shape=out_shape,
        in_specs=in_specs,
        out_specs=out_specs,
        scratch_shapes=scratch,
        compiler_params=pltpu.CompilerParams(
            collective_id=chunk, has_side_effects=True, vmem_limit_bytes=(60 if last else 24) * 1024 * 1024
        ),
        name=f"turn_{chunk}",
    )(*operands)


CHUNKS = 2


def body(ham, coeff, tile_mask, occupation, orbital_energy, coulomb):
    tile_rows, strings = ham.shape
    tile_cols = coeff.shape[1]
    mask_cols = tile_mask.shape[1]
    block_size = strings // mask_cols
    mask_rows = tile_rows // block_size
    weights = tile_mask.astype(jnp.bfloat16)[:, None, :, None]
    masked = (ham.reshape(mask_rows, block_size, mask_cols, block_size) * weights).reshape(
        tile_rows, strings
    )
    occ_float = occupation.astype(jnp.float32)
    occ_alpha = lax.dynamic_slice_in_dim(occ_float, lax.axis_index("row") * tile_rows, tile_rows, 1)
    occ_beta = lax.dynamic_slice_in_dim(occ_float, lax.axis_index("col") * tile_cols, tile_cols, 1)
    energy_alpha = jnp.dot(orbital_energy, occ_alpha, precision=HIGH)
    energy_beta = jnp.dot(orbital_energy, occ_beta, precision=HIGH)
    coupling = jnp.dot(jnp.dot(occ_alpha.T, coulomb, precision=HIGH), occ_beta, precision=HIGH)
    diagonal = energy_alpha[:, None] + energy_beta[None, :] + coupling
    fold = tile_cols // tile_rows
    chunks = math.gcd(CHUNKS, fold)
    products = []
    arrived = []
    for q in range(chunks):
        part = jnp.concatenate(
            [coeff[:, s * tile_rows : (s + 1) * tile_rows] for s in range(q, fold, chunks)], axis=1
        )
        gathered = with_layout_constraint(lax.all_gather(part, "row", axis=0, tiled=True), Layout((0, 1)))
        products.append(jnp.dot(masked, gathered, preferred_element_type=jnp.float32))
        result = turn(q, chunks, products, arrived, coeff, diagonal, strings)
        if q < chunks - 1:
            arrived.append(result)
    update, sums = result
    correction = update * lax.rsqrt(sums[2] + 1e-06)
    stats = jnp.stack([sums[0], jnp.sqrt(sums[1])])
    return (correction, stats)


def solution(mesh):
    in_specs = (P("row", None), P("row", "col"), P("row", None), P(), P(), P())
    out_specs = (P("row", "col"), P())
    return jax.shard_map(body, mesh=mesh, in_specs=in_specs, out_specs=out_specs, check_vma=False)
```

profile of v0, /device:TPU:0, one launch (start us, length us, event | category | flops | bytes accessed | tf_op | source)
XLA Modules:
  0.0 530.4 jit_solution(11912031971470785954)
XLA Ops:
  7.2 0.0 copy-start
  7.2 0.0 all-gather.3.cloned.1.call-start
  7.2 2.6 fusion.17
  9.8 0.0 copy-start.5
  9.8 1.6 pad_maximum_fusion
  11.5 0.0 all-gather.3.cloned.1.call-update
  11.5 0.0 all-gather.5.cloned.1.call-start
  11.5 1.6 pad_maximum_fusion.1
  13.2 0.0 all-gather.5.cloned.1.call-update
  13.2 0.0 copy-done.5
  13.2 12.3 %mul.23 = bf16[16,32,256,32]{3,2,1,0:T(8,128)(2,1)} broadcast(bf16[16,256]{1,0:T(8,128)(2,1)S(1)} %convert_element_type.6), dimensions={0,2} | broadcast | bytes 8396800 | tf_op jit(solution)/shard_map/mul | solution.py:424
  25.5 0.0 copy-start.4
  25.5 0.0 copy-start.6
  25.5 42.1 %mul.24 = bf16[512,8192]{1,0:T(8,128)(2,1)} reshape(bf16[16,32,256,32]{3,2,1,0:T(8,128)(2,1)} %mul.23) | data formatting | bytes 16777216 | tf_op jit(solution)/shard_map/mul | solution.py:424
  67.6 0.0 copy-done.4
  67.6 0.0 copy-done.6
  67.6 0.1 fusion.9
  67.8 0.3 fusion.5
  68.1 0.0 copy-done
  68.1 0.6 fusion.7
  68.7 9.0 %add_add_fusion.refs_3_ = f32[512,4096]{1,0:T(8,128)} fusion(f32[512,16]{1,0:T(8,128)S(1)} %fusion.7, f32[4096]{0:T(1024)S(1)} %bitcast.15, f32[512]{0:T(512)S(1)} %bitcast.16, f32[16,8192]{1,0:T(8,128)S(1)} %convert_element_type.7, s32[]{:T(128)S(6)} %select_n.7), kind=kOutput, calls=%fused_computation | convolution fusion | flops 406847488 | bytes 8931332 | tf_op jit(solution)/shard_map/dot_general | solution.py:432
  77.8 104.6 %all-gather.3.cloned.1.call-done = bf16[8192,2048]{1,0:T(8,128)(2,1)} async-done(((bf16[512,2048]{1,0:T(8,128)(2,1)}), bf16[8192,2048]{1,0:T(8,128)(2,1)}) %all-gather.3.cloned.1.call-update) | async-done | bytes 33554448 | tf_op jit(solution)/shard_map/all_gather | solution.py:442
  182.4 24.6 %fusion.2.refs_0_ = f32[512,2048]{1,0:T(8,128)S(1)} fusion(bf16[8192,2048]{1,0:T(8,128)(2,1)} %all-gather.3.cloned.1.call-done, bf16[512,8192]{1,0:T(8,128)(2,1)} %param.6, bf16[512,8192]{1,0:T(8,128)(2,1)} %mul.24), kind=kOutput, calls=%fused_computation.4 | convolution fusion | flops 17184063488 | bytes 54525952 | tf_op jit(solution)/shard_map/dot_general | solution.py:443
  207.1 102.5 %turn_0.1.refs_2_ = s16[8,2,272,512]{3,2,1,0:T(8,128)(2,1)S(1)} custom-call(f32[512,2048]{1,0:T(8,128)S(1)} %fusion.2.refs_0_), custom_call_target="tpu_custom_call" | custom-call | tf_op jit(solution)/shard_map/turn_0/pallas_call | solution.py:401
  309.6 0.0 copy-start.2
  309.6 2.1 copy-done.2
  311.7 0.0 copy-start.3
  311.7 2.0 copy-done.3
  313.7 86.1 %all-gather.5.cloned.1.call-done = bf16[8192,2048]{1,0:T(8,128)(2,1)} async-done(((bf16[512,2048]{1,0:T(8,128)(2,1)}), bf16[8192,2048]{1,0:T(8,128)(2,1)}) %all-gather.5.cloned.1.call-update) | async-done | bytes 33554448 | tf_op jit(solution)/shard_map/all_gather | solution.py:442
  399.8 27.2 %fusion.refs_1_ = f32[512,2048]{1,0:T(8,128)} fusion(bf16[8192,2048]{1,0:T(8,128)(2,1)} %all-gather.5.cloned.1.call-done, bf16[512,8192]{1,0:T(8,128)(2,1)} %param.6, bf16[512,8192]{1,0:T(8,128)(2,1)} %mul.24), kind=kOutput, calls=%fused_computation.2 | convolution fusion | flops 17184063488 | bytes 54525952 | tf_op jit(solution)/shard_map/dot_general | solution.py:443
  427.0 84.7 %turn_1.1 = (f32[512,4096]{1,0:T(8,128)}, f32[3]{0:T(128)}) custom-call(f32[512,2048]{1,0:T(8,128)} %copy-done.3, f32[512,2048]{1,0:T(8,128)} %fusion.refs_1_, s16[8,2,272,512]{3,2,1,0:T(8,128)(2,1)} %copy-done.2, f32[512,4096]{1,0:T(8,128)} %add_add_fusion.refs_3_, bf16[512,4096]{1,0:T(8,128)(2,1)} %refs_4_.1), custom_call_target="tpu_custom_call" | custom-call | tf_op jit(solution)/shard_map/turn_1/pallas_call | solution.py:401
  511.7 1.4 fusion.18
  514.5 0.0 copy-start.1
  514.5 7.9 %broadcast_multiply_fusion = f32[512,4096]{1,0:T(8,128)} fusion(f32[512,4096]{1,0:T(8,128)} %get-tuple-element.4, f32[]{:T(128)} %bitcast.4), kind=kLoop, calls=%fused_computation.1 | loop fusion | flops 2097152 | bytes 16777220 | tf_op jit(solution)/shard_map/mul | solution.py:448
  522.4 1.2 pad_maximum_fusion.2
  523.6 0.0 copy-done.1
  (2 shorter events, 0.0 us)
Async XLA Ops:
  7.2 60.9 %copy-start = (f32[16,16]{1,0:T(8,128)S(1)}, f32[16,16]{1,0:T(8,128)}, u32[]{:S(2)}) copy-start(f32[16,16]{1,0:T(8,128)} %param.11) | copy-start | bytes 3076
  7.2 175.2 %all-gather.3.cloned.1.call-start = ((), (), s32[]{:S(2)}) async-start(), calls=%async_computation | async-start | bytes 35651584 | tf_op jit(solution)/shard_map/all_gather | solution.py:442
  9.8 3.4 copy-start.5
  11.5 388.3 %all-gather.5.cloned.1.call-start = ((), (), s32[]{:S(2)}) async-start(), calls=%async_computation.1 | async-start | bytes 35651584 | tf_op jit(solution)/shard_map/all_gather | solution.py:442
  25.5 42.1 %copy-start.4 = (s32[16,8192]{1,0:T(8,128)S(1)}, s32[16,8192]{1,0:T(8,128)}, u32[]{:S(2)}) copy-start(s32[16,8192]{1,0:T(8,128)} %param.9) | copy-start | bytes 1572868
  25.5 42.2 %copy-start.6 = (f32[16]{0:T(128)S(1)}, f32[16]{0:T(128)}, u32[]{:S(2)}) copy-start(f32[16]{0:T(128)} %param.10) | copy-start | bytes 196
  309.6 2.1 copy-start.2
  311.7 2.0 copy-start.3
  514.5 9.1 %copy-start.1 = (f32[16,16]{1,0:T(8,128)S(1)}, f32[16,16]{1,0:T(8,128)}, u32[]{:S(2)}) copy-start(f32[16,16]{1,0:T(8,128)} %param.11) | copy-start | bytes 3076
Sparse Core Ops, SparseCore 0:
  11.6 170.7 all-gather.2
  184.0 215.7 all-gather.4
where the time goes:
time: 532 us; the launch traced here: 530 us
  waiting for transfers between devices  191 us (36%)
  Pallas kernels  187 us (35%)
  local copies, waits for them, and re-layouts  62.5 us (12%)
  matrix products  61.9 us (12%)
  between operations  15.5 us (3%)
  other arithmetic  12.4 us (2%)
    all_gather x2, waiting for transfers between devices, body(): lax.all_gather(part, 'row', axis=0, tiled=True)  191 us
    pallas_call x2, Pallas kernels, turn(): pl.pallas_call(functools.partial(turn_kernel, row_count, col_count, float...  187 us
    mul x2, local copies, waits for them, and re-layouts, body(): ham.reshape(mask_rows, block_size, mask_cols, block_size) * weights  54.4 us
    dot_general x2, matrix products, body(): jnp.dot(masked, gathered, preferred_element_type=jnp.float32)  51.9 us
  transfers between devices with their start and end apart: 2, of which 2 were waited for; matrix products, arithmetic and copies ran while one was open for 17% of the time, Pallas kernels for 19%

commit v1 on v0

--- a/solution.py
+++ b/solution.py
@@ -411,7 +411,7 @@
     )(*operands)
 
 
-CHUNKS = 2
+CHUNKS = 4
 
 
 def body(ham, coeff, tile_mask, occupation, orbital_energy, coulomb):

time: 532 us -> 699 us (1.31)
  waiting for transfers between devices: 191 us -> 280 us
  Pallas kernels: 187 us -> 243 us
  other arithmetic: 12.4 us -> 23.3 us
  matrix products: 61.9 us -> 69.6 us
    all_gather x2 -> x4, waiting for transfers between devices: 191 us -> 280 us  [body(): lax.all_gather(part, 'row', axis=0, tiled=True)]
    pallas_call x2 -> x4, Pallas kernels: 187 us -> 243 us  [turn(): pl.pallas_call(functools.partial(turn_kernel, row_count, col_count, float...]
    mul x0 -> x1, other arithmetic: none -> 9.57 us  [body(): ham.reshape(mask_rows, block_size, mask_cols, block_size) * weights]
    dot_general x2 -> x4, matrix products: 51.9 us -> 59.5 us  [body(): jnp.dot(masked, gathered, preferred_element_type=jnp.float32)]
  transfers between devices with their start and end apart: 2 -> 4, of which waited for: 2 -> 4; matrix products, arithmetic and copies ran while one was open for 17% -> 17% of each run, Pallas kernels for 19% -> 25%
where the time goes in v1:
time: 699 us; the launch traced here: 697 us
  waiting for transfers between devices  280 us (40%)
  Pallas kernels  243 us (35%)
  matrix products  69.6 us (10%)
  local copies, waits for them, and re-layouts  65.7 us (9%)
  other arithmetic  23.3 us (3%)
  between operations  15.3 us (2%)
    all_gather x4, waiting for transfers between devices, body(): lax.all_gather(part, 'row', axis=0, tiled=True)  280 us
    pallas_call x4, Pallas kernels, turn(): pl.pallas_call(functools.partial(turn_kernel, row_count, col_count, float...  243 us
    dot_general x4, matrix products, body(): jnp.dot(masked, gathered, preferred_element_type=jnp.float32)  59.5 us
    mul x2, local copies, waits for them, and re-layouts, body(): ham.reshape(mask_rows, block_size, mask_cols, block_size) * weights  54 us
  transfers between devices with their start and end apart: 4, of which 4 were waited for; matrix products, arithmetic and copies ran while one was open for 17% of the time, Pallas kernels for 25%

profile of v1, /device:TPU:0, one launch (start us, length us, event | category | flops | bytes accessed | tf_op | source)
XLA Modules:
  0.0 697.3 jit_solution(14694445216406036987)
XLA Ops:
  7.2 0.0 copy-start
  7.2 0.0 all-gather.5.cloned.1.call-start
  7.2 2.6 fusion.13
  9.8 0.0 copy-start.9
  9.9 1.1 pad_maximum_fusion
  11.0 0.0 all-gather.5.cloned.1.call-update
  11.0 0.0 all-gather.7.cloned.1.call-start
  11.1 1.1 pad_maximum_fusion.1
  12.2 0.0 all-gather.7.cloned.1.call-update
  12.2 0.0 all-gather.9.cloned.1.call-start
  12.3 1.1 pad_maximum_fusion.2
  13.4 0.0 all-gather.9.cloned.1.call-update
  13.4 0.0 all-gather.11.cloned.1.call-start
  13.5 1.2 pad_maximum_fusion.3
  14.6 0.0 all-gather.11.cloned.1.call-update
  14.7 0.0 copy-done.9
  14.7 12.0 %mul.23 = bf16[16,32,256,32]{3,2,1,0:T(8,128)(2,1)} broadcast(bf16[16,256]{1,0:T(8,128)(2,1)S(1)} %convert_element_type.6), dimensions={0,2} | broadcast | bytes 8396800 | tf_op jit(solution)/shard_map/mul | solution.py:424
  26.7 0.0 copy-start.8
  26.7 42.1 %mul.24 = bf16[512,8192]{1,0:T(8,128)(2,1)} reshape(bf16[16,32,256,32]{3,2,1,0:T(8,128)(2,1)} %mul.23) | data formatting | bytes 16777216 | tf_op jit(solution)/shard_map/mul | solution.py:424
  68.7 0.0 copy-done.8
  68.8 0.0 copy-start.10
  68.8 9.6 %mul.25 = bf16[512,8192]{1,0:T(8,128)(2,1)} multiply(bf16[512,8192]{1,0:T(8,128)(2,1)} %param.6, bf16[512,8192]{1,0:T(8,128)(2,1)} %mul.24) | non-fusion elementwise | flops 4194304 | bytes 25165824 | tf_op jit(solution)/shard_map/mul | solution.py:424
  78.3 0.0 copy-done.10
  78.4 0.1 fusion.5
  78.5 0.3 fusion.1
  78.8 0.0 copy-done
  78.8 0.6 fusion.3
  79.4 9.0 %add_add_fusion.refs_7_ = f32[512,4096]{1,0:T(8,128)} fusion(f32[512,16]{1,0:T(8,128)S(1)} %fusion.3, f32[4096]{0:T(1024)S(1)} %bitcast.21, f32[512]{0:T(512)S(1)} %bitcast.22, f32[16,8192]{1,0:T(8,128)S(1)} %convert_element_type.7, s32[]{:T(128)S(6)} %select_n.7), kind=kOutput, calls=%fused_computation | convolution fusion | flops 406847488 | bytes 8931332 | tf_op jit(solution)/shard_map/dot_general | solution.py:432
  88.4 51.9 %all-gather.5.cloned.1.call-done = bf16[8192,1024]{1,0:T(8,128)(2,1)} async-done(((bf16[512,1024]{1,0:T(8,128)(2,1)}), bf16[8192,1024]{1,0:T(8,128)(2,1)}) %all-gather.5.cloned.1.call-update) | async-done | bytes 16777232 | tf_op jit(solution)/shard_map/all_gather | solution.py:442
  140.3 14.6 %fusion.15.refs_0_ = f32[512,1024]{1,0:T(8,128)S(1)} fusion(bf16[512,8192]{1,0:T(8,128)(2,1)} %mul.25, bf16[8192,1024]{1,0:T(8,128)(2,1)} %all-gather.5.cloned.1.call-done), kind=kOutput, calls=%fused_computation.22 | convolution fusion | flops 8589934592 | bytes 27262976 | tf_op jit(solution)/shard_map/dot_general | solution.py:443
  154.9 0.0 copy-start.5
  154.9 67.1 %turn_0.1.refs_4_ = s16[8,2,272,512]{3,2,1,0:T(8,128)(2,1)S(1)} custom-call(f32[512,1024]{1,0:T(8,128)S(1)} %fusion.15.refs_0_), custom_call_target="tpu_custom_call" | custom-call | tf_op jit(solution)/shard_map/turn_0/pallas_call | solution.py:401
  222.1 0.0 copy-start.2
  222.1 2.0 copy-done.2
  224.1 66.9 %all-gather.7.cloned.1.call-done = bf16[8192,1024]{1,0:T(8,128)(2,1)} async-done(((bf16[512,1024]{1,0:T(8,128)(2,1)}), bf16[8192,1024]{1,0:T(8,128)(2,1)}) %all-gather.7.cloned.1.call-update) | async-done | bytes 16777232 | tf_op jit(solution)/shard_map/all_gather | solution.py:442
  291.0 14.6 %fusion.16.refs_0_.refs_1_ = f32[512,1024]{1,0:T(8,128)S(1)} fusion(bf16[512,8192]{1,0:T(8,128)(2,1)} %mul.25, bf16[8192,1024]{1,0:T(8,128)(2,1)} %all-gather.7.cloned.1.call-done), kind=kOutput, calls=%fused_computation.23 | convolution fusion | flops 8589934592 | bytes 27262976 | tf_op jit(solution)/shard_map/dot_general | solution.py:443
  305.6 0.0 copy-done.5
  305.6 52.4 %turn_1.1.refs_5_ = s16[8,2,272,512]{3,2,1,0:T(8,128)(2,1)S(1)} custom-call(f32[512,1024]{1,0:T(8,128)S(1)} %fusion.16.refs_0_.refs_1_), custom_call_target="tpu_custom_call" | custom-call | tf_op jit(solution)/shard_map/turn_1/pallas_call | solution.py:401
  358.0 0.0 copy-start.3
  358.0 2.1 copy-done.3
  360.1 0.0 copy-start.6
  360.1 1.3 copy-done.6
  361.5 80.2 %all-gather.9.cloned.1.call-done = bf16[8192,1024]{1,0:T(8,128)(2,1)} async-done(((bf16[512,1024]{1,0:T(8,128)(2,1)}), bf16[8192,1024]{1,0:T(8,128)(2,1)}) %all-gather.9.cloned.1.call-update) | async-done | bytes 16777232 | tf_op jit(solution)/shard_map/all_gather | solution.py:442
  441.7 14.6 %fusion.17.refs_0_.refs_2_ = f32[512,1024]{1,0:T(8,128)S(1)} fusion(bf16[512,8192]{1,0:T(8,128)(2,1)} %mul.25, bf16[8192,1024]{1,0:T(8,128)(2,1)} %all-gather.9.cloned.1.call-done), kind=kOutput, calls=%fused_computation.24 | convolution fusion | flops 8589934592 | bytes 27262976 | tf_op jit(solution)/shard_map/dot_general | solution.py:443
  456.3 0.0 copy-start.7
  456.3 52.4 %turn_2.1.refs_6_ = s16[8,2,272,512]{3,2,1,0:T(8,128)(2,1)S(1)} custom-call(f32[512,1024]{1,0:T(8,128)S(1)} %fusion.17.refs_0_.refs_2_), custom_call_target="tpu_custom_call" | custom-call | tf_op jit(solution)/shard_map/turn_2/pallas_call | solution.py:401
  508.7 0.0 copy-start.4
  508.7 2.1 copy-done.4
  510.9 81.4 %all-gather.11.cloned.1.call-done = bf16[8192,1024]{1,0:T(8,128)(2,1)} async-done(((bf16[512,1024]{1,0:T(8,128)(2,1)}), bf16[8192,1024]{1,0:T(8,128)(2,1)}) %all-gather.11.cloned.1.call-update) | async-done | bytes 16777232 | tf_op jit(solution)/shard_map/all_gather | solution.py:442
  592.2 15.8 %fusion.18.refs_3_ = f32[512,1024]{1,0:T(8,128)} fusion(bf16[512,8192]{1,0:T(8,128)(2,1)} %mul.25, bf16[8192,1024]{1,0:T(8,128)(2,1)} %all-gather.11.cloned.1.call-done), kind=kOutput, calls=%fused_computation.25 | convolution fusion | flops 8589934592 | bytes 27262976 | tf_op jit(solution)/shard_map/dot_general | solution.py:443
  608.0 0.0 copy-done.7
  608.0 70.8 %turn_3.1 = (f32[512,4096]{1,0:T(8,128)}, f32[3]{0:T(128)}) custom-call(f32[512,1024]{1,0:T(8,128)} %copy-done.5, f32[512,1024]{1,0:T(8,128)} %copy-done.6, f32[512,1024]{1,0:T(8,128)} %copy-done.7, f32[512,1024]{1,0:T(8,128)} %fusion.18.refs_3_, s16[8,2,272,512]{3,2,1,0:T(8,128)(2,1)} %copy-done.2, s16[8,2,272,512]{3,2,1,0:T(8,128)(2,1)} %copy-done.3, ...), custom_call_target="tpu_custom_call" | custom-call | tf_op jit(solution)/shard_map/turn_3/pallas_call | solution.py:401
  678.9 1.4 fusion.14
  681.6 0.0 copy-start.1
  681.6 7.9 %broadcast_multiply_fusion = f32[512,4096]{1,0:T(8,128)} fusion(f32[512,4096]{1,0:T(8,128)} %get-tuple-element.4, f32[]{:T(128)} %bitcast.4), kind=kLoop, calls=%fused_computation.1 | loop fusion | flops 2097152 | bytes 16777220 | tf_op jit(solution)/shard_map/mul | solution.py:448
  689.5 1.3 pad_maximum_fusion.4
  690.8 0.0 copy-done.1
  (2 shorter events, 0.0 us)
Async XLA Ops:
  7.2 71.6 %copy-start = (f32[16,16]{1,0:T(8,128)S(1)}, f32[16,16]{1,0:T(8,128)}, u32[]{:S(2)}) copy-start(f32[16,16]{1,0:T(8,128)} %param.11) | copy-start | bytes 3076
  7.2 133.2 %all-gather.5.cloned.1.call-start = ((), (), s32[]{:S(2)}) async-start(), calls=%async_computation | async-start | bytes 17825792 | tf_op jit(solution)/shard_map/all_gather | solution.py:442
  9.8 4.8 copy-start.9
  11.0 280.0 %all-gather.7.cloned.1.call-start = ((), (), s32[]{:S(2)}) async-start(), calls=%async_computation.1 | async-start | bytes 17825792 | tf_op jit(solution)/shard_map/all_gather | solution.py:442
  12.2 429.4 %all-gather.9.cloned.1.call-start = ((), (), s32[]{:S(2)}) async-start(), calls=%async_computation.2 | async-start | bytes 17825792 | tf_op jit(solution)/shard_map/all_gather | solution.py:442
  13.4 578.8 %all-gather.11.cloned.1.call-start = ((), (), s32[]{:S(2)}) async-start(), calls=%async_computation.3 | async-start | bytes 17825792 | tf_op jit(solution)/shard_map/all_gather | solution.py:442
  26.7 42.1 %copy-start.8 = (s32[16,8192]{1,0:T(8,128)S(1)}, s32[16,8192]{1,0:T(8,128)}, u32[]{:S(2)}) copy-start(s32[16,8192]{1,0:T(8,128)} %param.9) | copy-start | bytes 1572868
  68.8 9.6 %copy-start.10 = (f32[16]{0:T(128)S(1)}, f32[16]{0:T(128)}, u32[]{:S(2)}) copy-start(f32[16]{0:T(128)} %param.10) | copy-start | bytes 196
  154.9 150.7 %copy-start.5 = (f32[512,1024]{1,0:T(8,128)}, f32[512,1024]{1,0:T(8,128)S(1)}, u32[]{:S(2)}) copy-start(f32[512,1024]{1,0:T(8,128)S(1)} %fusion.15.refs_0_) | copy-start | bytes 6291460
  222.1 2.0 copy-start.2
  358.0 2.1 copy-start.3
  360.1 1.3 copy-start.6
  456.3 151.8 %copy-start.7 = (f32[512,1024]{1,0:T(8,128)}, f32[512,1024]{1,0:T(8,128)S(1)}, u32[]{:S(2)}) copy-start(f32[512,1024]{1,0:T(8,128)S(1)} %fusion.17.refs_0_.refs_2_) | copy-start | bytes 6291460
  508.7 2.2 copy-start.4
  681.6 9.1 %copy-start.1 = (f32[16,16]{1,0:T(8,128)S(1)}, f32[16,16]{1,0:T(8,128)}, u32[]{:S(2)}) copy-start(f32[16,16]{1,0:T(8,128)} %param.11) | copy-start | bytes 3076
Sparse Core Ops, SparseCore 0:
  11.1 129.1 all-gather.4
  142.5 148.4 all-gather.6
  293.2 148.4 all-gather.8
  443.7 148.4 all-gather.10

commit v2 on v0

--- a/solution.py
+++ b/solution.py
@@ -411,19 +411,391 @@
     )(*operands)
 
 
+def gather_kernel(ham_ref, mask_ref, coeff_ref, ring_ref, acc_ref, wide, ring, m_ref, buf, load_sem, send_sem, wide_sem, ring_sem):
+    rows, strings = ham_ref.shape
+    half = coeff_ref.shape[1]
+    quarter = rows // 4
+    row = lax.axis_index("row")
+    col = lax.axis_index("col")
+    core = lax.rem(row, 2)
+    x = lax.rem(lax.div(row, 2), 2)
+    low = lax.rem(lax.div(row, 4), 2)
+    high = lax.div(row, 8)
+    diag = high == col
+    mid = low != high
+    fold = half // rows
+
+    def device(h, l, a, k):
+        return ((h * 2 + l) * 2 + a) * 2 + k
+
+    targets = {
+        "x": (device(high, low, 1 - x, core), col),
+        "z": (device(high, 1 - low, x, core), col),
+        "y": (row, 1 - col),
+        "c": (device(high, low, x, 1 - core), col),
+        "cut": (device(1 - high, 1 - low, x, core), col),
+    }
+
+    ham_load = pltpu.make_async_copy(ham_ref, m_ref, load_sem.at[0])
+    ham_load.start()
+
+    barrier = pltpu.get_barrier_semaphore()
+    for target in targets.values():
+        pl.semaphore_signal(barrier, inc=1, device_id=target, device_id_type=MESH)
+    pl.semaphore_wait(barrier, len(targets))
+
+    def spot(l, a, k):
+        return (l * 2 + a) * 2 + k
+
+    def part(ref, t, q):
+        return ref.at[t, pl.ds(q * quarter, quarter)]
+
+    sent = []
+
+    def send(way, ref, sems, t, q, own=None):
+        src = part(ref, t, q) if own is None else own.at[pl.ds(q * quarter, quarter)]
+        copy = pltpu.make_async_remote_copy(
+            src_ref=src,
+            dst_ref=part(ref, t, q),
+            send_sem=send_sem.at[len(sent)],
+            recv_sem=sems.at[t, q],
+            device_id=targets[way],
+            device_id_type=MESH,
+        )
+        sent.append((copy, way == "cut"))
+        if way == "cut":
+
+            @pl.when(mid)
+            def _():
+                copy.start()
+        else:
+            copy.start()
+
+    def settle():
+        for copy, only_mid in sent:
+            if only_mid:
+
+                @pl.when(mid)
+                def _():
+                    copy.wait_send()
+            else:
+                copy.wait_send()
+        sent.clear()
+
+    def arrive(ref, sems, t, q):
+        view = part(ref, t, q)
+        pltpu.make_async_copy(view, view, sems.at[t, q]).wait()
+
+    def pass_on(ref, sems, t, q, *ways):
+        arrive(ref, sems, t, q)
+        for way in ways:
+            send(way, ref, sems, t, q)
+        send("c", ref, sems, t, q)
+
+    def load(ref, sems, l, a, width, own=None):
+        mine, other = spot(l, a, core), spot(l, a, 1 - core)
+        for q in range(4):
+            arrive(ref, sems, other, q)
+        src = ref.at[mine] if own is None else own
+        first = pltpu.make_async_copy(
+            src, buf.at[pl.ds(pl.multiple_of(core * rows, rows), rows), pl.ds(0, width)], load_sem.at[1]
+        )
+        second = pltpu.make_async_copy(
+            ref.at[other],
+            buf.at[pl.ds(pl.multiple_of((1 - core) * rows, rows), rows), pl.ds(0, width)],
+            load_sem.at[2],
+        )
+        first.start()
+        second.start()
+        first.wait()
+        second.wait()
+
+    def block(n):
+        return pl.ds(pl.multiple_of(n * rows, rows), rows)
+
+    near = col * fold
+    away = (1 - col) * fold
+
+    def plain(l, a):
+        base = spot(l, a, 0)
+        left = pl.ds(pl.multiple_of((away + base) * rows, rows), 2 * rows)
+
+        def one(n, carry):
+            acc_ref[:, block(n)] += jnp.dot(m_ref[:, left], buf[:, block(n)], preferred_element_type=jnp.float32)
+            return carry
+
+        lax.fori_loop(0, fold, one, 0)
+
+    def turned(l, a):
+        base = spot(l, a, 0)
+
+        def one(n, carry):
+            total = jnp.zeros((rows, rows), jnp.float32)
+            for k in range(0, fold, 2):
+                left = pl.ds(pl.multiple_of((away + k) * rows, rows), 2 * rows)
+                total = total + lax.dot_general(
+                    m_ref[:, left],
+                    buf[block(n), pl.ds(k * rows, 2 * rows)],
+                    (((1,), (1,)), ((), ())),
+                    preferred_element_type=jnp.float32,
+                )
+            acc_ref[:, block(base + n)] += total
+            return carry
+
+        lax.fori_loop(0, 2, one, 0)
+
+    def mirrored(l, a):
+        base = spot(l, a, 0)
+
+        def lane(k, carry):
+            t = base + k
+
+            def one(d, inner):
+                s = lax.rem(t + d, fold)
+                tile = buf[block(k), block(d)]
+                acc_ref[:, block(s)] += jnp.dot(
+                    m_ref[:, block(near + t)], tile, preferred_element_type=jnp.float32
+                )
+
+                @pl.when(d > 0)
+                def _():
+                    acc_ref[:, block(t)] += lax.dot_general(
+                        m_ref[:, block(near + s)],
+                        tile,
+                        (((1,), (1,)), ((), ())),
+                        preferred_element_type=jnp.float32,
+                    )
+
+                return inner
+
+            last = jnp.where(t < fold // 2, fold // 2 + 1, fold // 2)
+            lax.fori_loop(0, last, one, 0)
+            return carry
+
+        lax.fori_loop(0, 2, lane, 0)
+
+    def prepare():
+        ham_load.wait()
+        groups, blocks = mask_ref.shape
+        size = strings // blocks
+        step = min(1024, strings)
+        pick = lax.broadcasted_iota(jnp.int32, (rows, groups), 0) // size == lax.broadcasted_iota(
+            jnp.int32, (rows, groups), 1
+        )
+        tall = jnp.dot(
+            pick.astype(jnp.bfloat16), mask_ref[...].astype(jnp.bfloat16), preferred_element_type=jnp.float32
+        ).astype(jnp.bfloat16)
+
+        def one(n, carry):
+            cols = pl.ds(pl.multiple_of(n * step, step), step)
+            spread = (n * step + lax.broadcasted_iota(jnp.int32, (blocks, step), 1)) // size == lax.broadcasted_iota(
+                jnp.int32, (blocks, step), 0
+            )
+            weight = jnp.dot(tall, spread.astype(jnp.bfloat16), preferred_element_type=jnp.float32)
+            m_ref[:, cols] = m_ref[:, cols] * weight.astype(jnp.bfloat16)
+            acc_ref[:, pl.ds(pl.multiple_of(n * (step // 2), step // 2), step // 2)] = jnp.zeros(
+                (rows, step // 2), jnp.float32
+            )
+            return carry
+
+        lax.fori_loop(0, strings // step, one, 0)
+
+    reach = ring.shape[2]
+    W = (wide, wide_sem)
+    R = (ring, ring_sem)
+    own = spot(low, x, core)
+    t_x = spot(low, 1 - x, core)
+    t_z = spot(1 - low, x, core)
+    t_d = spot(1 - low, 1 - x, core)
+
+    @pl.when(diag)
+    def _():
+        def mine(q):
+            for way in ("x", "z", "cut", "c"):
+                send(way, *R, own, q, ring_ref)
+
+        mine(0)
+        mine(1)
+        prepare()
+        pass_on(*R, t_z, 0, "cut")
+        pass_on(*R, t_x, 0, "z")
+        pass_on(*W, own, 0, "z")
+        mine(2)
+        pass_on(*R, t_z, 1, "cut")
+        pass_on(*R, t_x, 1, "z")
+        pass_on(*W, t_x, 0, "z")
+        pass_on(*W, t_z, 0, "y")
+        mine(3)
+        pass_on(*W, t_z, 2, "x")
+        pass_on(*W, t_d, 0, "y")
+        pass_on(*R, t_z, 2, "x", "cut")
+        pass_on(*R, t_x, 2)
+        pass_on(*W, own, 3, "x")
+        pass_on(*W, t_d, 2, "y")
+        pass_on(*R, t_z, 3, "x", "cut")
+        pass_on(*R, t_x, 3)
+        load(*R, low, x, reach, ring_ref)
+        mirrored(low, x)
+        pass_on(*W, t_x, 1, "z")
+        pass_on(*W, t_x, 3, "y")
+        load(*R, 1 - low, x, reach)
+        mirrored(1 - low, x)
+        pass_on(*W, t_z, 3, "x")
+        pass_on(*W, t_d, 1, "y")
+        for q in range(4):
+            pass_on(*R, t_d, q)
+        load(*R, low, 1 - x, reach)
+        mirrored(low, 1 - x)
+        pass_on(*W, own, 1, "z")
+        pass_on(*W, t_d, 3, "y")
+        load(*R, 1 - low, 1 - x, reach)
+        mirrored(1 - low, 1 - x)
+        pass_on(*W, own, 2, "x")
+        load(*W, 1 - low, 1 - x, half)
+        turned(1 - low, 1 - x)
+        pass_on(*W, t_z, 1)
+        pass_on(*W, t_x, 2)
+        load(*W, low, x, half)
+        turned(low, x)
+        load(*W, 1 - low, x, half)
+        turned(1 - low, x)
+        load(*W, low, 1 - x, half)
+        turned(low, 1 - x)
+        settle()
+
+    @pl.when(jnp.logical_not(diag))
+    def _():
+        def mine(way, q):
+            send(way, *W, own, q, coeff_ref)
+
+        mine("y", 0)
+        mine("x", 0)
+        mine("z", 2)
+        mine("x", 1)
+        mine("z", 3)
+        mine("x", 2)
+        mine("z", 1)
+        for q in range(4):
+            mine("c", q)
+        pass_on(*W, t_x, 0, "y")
+        pass_on(*W, t_z, 2, "y")
+        mine("y", 3)
+        prepare()
+        pass_on(*W, t_x, 1, "y")
+        pass_on(*W, t_z, 3, "y")
+        mine("y", 1)
+        mine("y", 2)
+        front = 1 - col
+        back = col
+        a_own, b_own = spot(front, x, core), spot(back, x, core)
+        a_far, b_far = spot(front, 1 - x, core), spot(back, 1 - x, core)
+
+        def inward(t, q):
+            arrive(*R, t, q)
+            send("x", *R, t, q)
+            copy = pltpu.make_async_remote_copy(
+                src_ref=part(ring, t, q),
+                dst_ref=part(ring, t, q),
+                send_sem=send_sem.at[len(sent)],
+                recv_sem=ring_sem.at[t, q],
+                device_id=targets["z"],
+                device_id_type=MESH,
+            )
+            sent.append((copy, True))
+
+            @pl.when(mid)
+            def _():
+                copy.start()
+
+            send("c", *R, t, q)
+
+        load(*W, low, x, half, coeff_ref)
+        plain(low, x)
+        inward(a_own, 0)
+        pass_on(*W, t_x, 2)
+        pass_on(*W, t_z, 1)
+        inward(b_own, 0)
+        pass_on(*W, t_z, 0)
+        inward(a_own, 1)
+        inward(b_own, 1)
+        pass_on(*W, t_d, 0)
+        pass_on(*R, a_far, 0)
+        pass_on(*W, t_d, 2)
+        inward(a_own, 2)
+        pass_on(*R, b_far, 0)
+        inward(b_own, 2)
+        load(*W, 1 - low, x, half)
+        plain(1 - low, x)
+        pass_on(*W, t_x, 3)
+        pass_on(*R, a_far, 1)
+        inward(a_own, 3)
+        pass_on(*R, b_far, 1)
+        load(*W, low, 1 - x, half)
+        plain(low, 1 - x)
+        pass_on(*W, t_d, 1)
+        inward(b_own, 3)
+        pass_on(*R, a_far, 2)
+        load(*R, front, x, reach)
+        mirrored(front, x)
+        pass_on(*R, b_far, 2)
+        pass_on(*W, t_d, 3)
+        load(*R, back, x, reach)
+        mirrored(back, x)
+        pass_on(*R, a_far, 3)
+        pass_on(*R, b_far, 3)
+        load(*W, 1 - low, 1 - x, half)
+        plain(1 - low, 1 - x)
+        load(*R, front, 1 - x, reach)
+        mirrored(front, 1 - x)
+        load(*R, back, 1 - x, reach)
+        mirrored(back, 1 - x)
+        settle()
+
+
+def gather_products(ham, tile_mask, coeff):
+    rows, strings = ham.shape
+    half = coeff.shape[1]
+    fold = half // rows
+    row = lax.axis_index("row")
+    reach = (fold // 2 + 1) * rows
+    start = jnp.where(lax.div(row, fold) == lax.axis_index("col"), lax.rem(row, fold) * rows, 0)
+    doubled = jnp.concatenate([coeff, coeff[:, : reach - rows]], axis=1)
+    ring = lax.dynamic_slice(doubled, (0, start), (rows, reach))
+    anywhere = pl.BlockSpec(memory_space=pl.ANY)
+    vmem = pl.BlockSpec(memory_space=pltpu.VMEM)
+    dma = pltpu.SemaphoreType.DMA
+    return pl.pallas_call(
+        gather_kernel,
+        out_shape=(
+            jax.ShapeDtypeStruct((rows, half), jnp.float32),
+            jax.ShapeDtypeStruct((fold, rows, half), jnp.bfloat16),
+            jax.ShapeDtypeStruct((fold, rows, reach), jnp.bfloat16),
+        ),
+        in_specs=[anywhere, vmem, anywhere, anywhere],
+        out_specs=(vmem, anywhere, anywhere),
+        scratch_shapes=[
+            pltpu.VMEM((rows, strings), jnp.bfloat16),
+            pltpu.VMEM((2 * rows, half), jnp.bfloat16),
+            dma((3,)),
+            dma((80,)),
+            dma((fold, 4)),
+            dma((fold, 4)),
+        ],
+        compiler_params=pltpu.CompilerParams(
+            collective_id=9, has_side_effects=True, vmem_limit_bytes=50 * 1024 * 1024
+        ),
+        name="gather_products",
+    )(ham, tile_mask, coeff, ring)[0]
+
+
 CHUNKS = 2
 
 
 def body(ham, coeff, tile_mask, occupation, orbital_energy, coulomb):
     tile_rows, strings = ham.shape
     tile_cols = coeff.shape[1]
-    mask_cols = tile_mask.shape[1]
-    block_size = strings // mask_cols
-    mask_rows = tile_rows // block_size
-    weights = tile_mask.astype(jnp.bfloat16)[:, None, :, None]
-    masked = (ham.reshape(mask_rows, block_size, mask_cols, block_size) * weights).reshape(
-        tile_rows, strings
-    )
+    fold = tile_cols // tile_rows
+    direct = lax.axis_size("col") == 2 and lax.axis_size("row") == 16
     occ_float = occupation.astype(jnp.float32)
     occ_alpha = lax.dynamic_slice_in_dim(occ_float, lax.axis_index("row") * tile_rows, tile_rows, 1)
     occ_beta = lax.dynamic_slice_in_dim(occ_float, lax.axis_index("col") * tile_cols, tile_cols, 1)
@@ -431,19 +803,26 @@
     energy_beta = jnp.dot(orbital_energy, occ_beta, precision=HIGH)
     coupling = jnp.dot(jnp.dot(occ_alpha.T, coulomb, precision=HIGH), occ_beta, precision=HIGH)
     diagonal = energy_alpha[:, None] + energy_beta[None, :] + coupling
-    fold = tile_cols // tile_rows
-    chunks = math.gcd(CHUNKS, fold)
-    products = []
-    arrived = []
-    for q in range(chunks):
-        part = jnp.concatenate(
-            [coeff[:, s * tile_rows : (s + 1) * tile_rows] for s in range(q, fold, chunks)], axis=1
-        )
-        gathered = with_layout_constraint(lax.all_gather(part, "row", axis=0, tiled=True), Layout((0, 1)))
-        products.append(jnp.dot(masked, gathered, preferred_element_type=jnp.float32))
-        result = turn(q, chunks, products, arrived, coeff, diagonal, strings)
-        if q < chunks - 1:
-            arrived.append(result)
+    if direct:
+        result = turn(0, 1, [gather_products(ham, tile_mask, coeff)], [], coeff, diagonal, strings)
+    else:
+        mask_cols = tile_mask.shape[1]
+        block_size = strings // mask_cols
+        mask_rows = tile_rows // block_size
+        weights = tile_mask.astype(jnp.bfloat16)[:, None, :, None]
+        masked = (ham.reshape(mask_rows, block_size, mask_cols, block_size) * weights).reshape(tile_rows, strings)
+        chunks = math.gcd(CHUNKS, fold)
+        products = []
+        arrived = []
+        for q in range(chunks):
+            part = jnp.concatenate(
+                [coeff[:, s * tile_rows : (s + 1) * tile_rows] for s in range(q, fold, chunks)], axis=1
+            )
+            gathered = with_layout_constraint(lax.all_gather(part, "row", axis=0, tiled=True), Layout((0, 1)))
+            products.append(jnp.dot(masked, gathered, preferred_element_type=jnp.float32))
+            result = turn(q, chunks, products, arrived, coeff, diagonal, strings)
+            if q < chunks - 1:
+                arrived.append(result)
     update, sums = result
     correction = update * lax.rsqrt(sums[2] + 1e-06)
     stats = jnp.stack([sums[0], jnp.sqrt(sums[1])])

time: 532 us -> 436 us (0.82)
  Pallas kernels: 187 us -> 408 us
  waiting for transfers between devices: 191 us -> 0 us
  local copies, waits for them, and re-layouts: 62.5 us -> 3.26 us
  matrix products: 61.9 us -> 10.1 us
  between operations: 15.5 us -> 2.14 us
    pallas_call x0 -> x1, Pallas kernels: none -> 254 us  [gather_products(): pl.pallas_call(gather_kernel, out_shape=(jax.ShapeDtypeStruct((rows, half...]
    all_gather x2 -> x0, waiting for transfers between devices: 191 us -> none  [body(): lax.all_gather(part, 'row', axis=0, tiled=True)]
    mul x2 -> x0, local copies, waits for them, and re-layouts: 54.4 us -> none  [body(): ham.reshape(mask_rows, block_size, mask_cols, block_size) * weights]
    dot_general x2 -> x0, matrix products: 51.9 us -> none  [body(): jnp.dot(masked, gathered, preferred_element_type=jnp.float32)]
    pallas_call x2 -> x1, Pallas kernels: 187 us -> 153 us  [turn(): pl.pallas_call(functools.partial(turn_kernel, row_count, col_count, float...]
  transfers between devices with their start and end apart: 2 -> 0, of which waited for: 2 -> 0; matrix products, arithmetic and copies ran while one was open for 17% -> 0% of each run, Pallas kernels for 19% -> 0%
where the time goes in v2:
time: 436 us; the launch traced here: 435 us
  Pallas kernels  408 us (94%)
  other arithmetic  11.9 us (3%)
  matrix products  10.1 us (2%)
    pallas_call x1, Pallas kernels, gather_products(): pl.pallas_call(gather_kernel, out_shape=(jax.ShapeDtypeStruct((rows, half...  254 us
    pallas_call x1, Pallas kernels, turn(): pl.pallas_call(functools.partial(turn_kernel, row_count, col_count, float...  153 us
    dot_general x1, matrix products, body(): jnp.dot(jnp.dot(occ_alpha.T, coulomb, precision=HIGH), occ_beta, precisio...  9.07 us

profile of v2, /device:TPU:0, one launch (start us, length us, event | category | flops | bytes accessed | tf_op | source)
XLA Modules:
  0.0 435.1 jit_solution(3503477560988895182)
XLA Ops:
  0.6 0.0 copy-start
  0.6 0.0 copy-start.2
  0.7 1.8 slice.12
  2.5 2.8 fusion.ring_ref
  5.3 0.0 copy-done.2
  5.3 0.0 copy-start.3
  5.4 0.0 copy-start.4
  5.4 254.4 %gather_products.1 = (f32[512,4096]{1,0:T(8,128)}, bf16[8,512,4096]{2,1,0:T(8,128)(2,1)}, bf16[8,512,2560]{2,1,0:T(8,128)(2,1)}) custom-call(bf16[512,8192]{1,0:T(8,128)(2,1)} %ham_ref.1, s32[16,256]{1,0:T(8,128)S(1)} %copy-done.2, bf16[512,4096]{1,0:T(8,128)(2,1)} %refs_2_.1, bf16[512,2560]{1,0:T(8,128)(2,1)S(1)} %fusion.ring_ref), custom_call_target="tpu_custom_call" | custom-call | tf_op jit(solution)/shard_map/gather_products/pallas_call | solution.py:767
  259.8 0.0 copy-done.3
  259.8 0.0 copy-done
  259.9 0.6 fusion.4
  260.5 0.0 copy-done.4
  260.5 0.1 fusion.6
  260.6 0.3 fusion.2
  260.9 9.1 %add_add_fusion.refs_1_ = f32[512,4096]{1,0:T(8,128)} fusion(f32[512,16]{1,0:T(8,128)S(1)} %fusion.4, f32[4096]{0:T(1024)S(1)} %bitcast.11, f32[512]{0:T(512)S(1)} %bitcast.12, f32[16,8192]{1,0:T(8,128)S(1)} %convert_element_type.3, s32[]{:T(128)S(6)} %select_n.16), kind=kOutput, calls=%fused_computation | convolution fusion | flops 406847488 | bytes 8931332 | tf_op jit(solution)/shard_map/dot_general | solution.py:804
  270.0 153.3 %turn_0.1 = (f32[512,4096]{1,0:T(8,128)}, f32[3]{0:T(128)}) custom-call(f32[512,4096]{1,0:T(8,128)} %get-tuple-element.5.refs_0_, f32[512,4096]{1,0:T(8,128)} %add_add_fusion.refs_1_, bf16[512,4096]{1,0:T(8,128)(2,1)} %refs_2_.1), custom_call_target="tpu_custom_call" | custom-call | tf_op jit(solution)/shard_map/turn_0/pallas_call | solution.py:401
  423.2 1.4 fusion.14
  425.3 1.2 pad_maximum_fusion
  427.2 0.0 copy-start.1
  427.2 7.9 %broadcast_multiply_fusion = f32[512,4096]{1,0:T(8,128)} fusion(f32[512,4096]{1,0:T(8,128)} %get-tuple-element.6, f32[]{:T(128)} %bitcast.4), kind=kLoop, calls=%fused_computation.3 | loop fusion | flops 2097152 | bytes 16777220 | tf_op jit(solution)/shard_map/mul | solution.py:827
  435.1 0.0 copy-done.1
  (1 shorter events, 0.0 us)
Async XLA Ops:
  0.6 259.2 %copy-start = (f32[16,16]{1,0:T(8,128)S(1)}, f32[16,16]{1,0:T(8,128)}, u32[]{:S(2)}) copy-start(f32[16,16]{1,0:T(8,128)} %param.11) | copy-start | bytes 3076
  0.6 4.7 %copy-start.2 = (s32[16,256]{1,0:T(8,128)S(1)}, s32[16,256]{1,0:T(8,128)}, u32[]{:S(2)}) copy-start(s32[16,256]{1,0:T(8,128)} %mask_ref.1) | copy-start | bytes 49156
  5.3 254.4 %copy-start.3 = (s32[16,8192]{1,0:T(8,128)S(1)}, s32[16,8192]{1,0:T(8,128)}, u32[]{:S(2)}) copy-start(s32[16,8192]{1,0:T(8,128)} %param.9) | copy-start | bytes 1572868
  5.4 255.1 %copy-start.4 = (f32[16]{0:T(128)S(1)}, f32[16]{0:T(128)}, u32[]{:S(2)}) copy-start(f32[16]{0:T(128)} %param.10) | copy-start | bytes 196
  427.2 7.9 %copy-start.1 = (f32[16,16]{1,0:T(8,128)S(1)}, f32[16,16]{1,0:T(8,128)}, u32[]{:S(2)}) copy-start(f32[16,16]{1,0:T(8,128)} %param.11) | copy-start | bytes 3076

commit v3 on v2

--- a/solution.py
+++ b/solution.py
@@ -411,7 +411,26 @@
     )(*operands)
 
 
-def gather_kernel(ham_ref, mask_ref, coeff_ref, ring_ref, acc_ref, wide, ring, m_ref, buf, load_sem, send_sem, wide_sem, ring_sem):
+def gather_kernel(
+    ham_ref,
+    mask_ref,
+    coeff_ref,
+    ring_ref,
+    couple_ref,
+    occ_ref,
+    alpha_ref,
+    beta_ref,
+    acc_ref,
+    wide,
+    ring,
+    diagonal_ref,
+    m_ref,
+    buf,
+    load_sem,
+    send_sem,
+    wide_sem,
+    ring_sem,
+):
     rows, strings = ham_ref.shape
     half = coeff_ref.shape[1]
     quarter = rows // 4
@@ -450,10 +469,13 @@
     def part(ref, t, q):
         return ref.at[t, pl.ds(q * quarter, quarter)]
 
+    end = jnp.logical_not(mid)
     sent = []
 
-    def send(way, ref, sems, t, q, own=None):
+    def send(way, ref, sems, t, q, own=None, when=None):
         src = part(ref, t, q) if own is None else own.at[pl.ds(q * quarter, quarter)]
+        if way == "cut":
+            when = mid
         copy = pltpu.make_async_remote_copy(
             src_ref=src,
             dst_ref=part(ref, t, q),
@@ -462,24 +484,25 @@
             device_id=targets[way],
             device_id_type=MESH,
         )
-        sent.append((copy, way == "cut"))
-        if way == "cut":
-
-            @pl.when(mid)
+        sent.append((copy, when))
+        if when is None:
+            copy.start()
+        else:
+
+            @pl.when(when)
             def _():
                 copy.start()
-        else:
-            copy.start()
 
     def settle():
-        for copy, only_mid in sent:
-            if only_mid:
-
-                @pl.when(mid)
+        for copy, when in sent:
+            if when is None:
+                copy.wait_send()
+            else:
+
+                @pl.when(when)
                 def _():
                     copy.wait_send()
-            else:
-                copy.wait_send()
+
         sent.clear()
 
     def arrive(ref, sems, t, q):
@@ -600,6 +623,17 @@
 
         lax.fori_loop(0, strings // step, one, 0)
 
+    def energies():
+        def one(n, carry):
+            diagonal_ref[:, block(n)] = (
+                jnp.dot(couple_ref[...], occ_ref[:, block(n)], precision=HIGH, preferred_element_type=jnp.float32)
+                + alpha_ref[...]
+                + beta_ref[:, block(n)]
+            )
+            return carry
+
+        lax.fori_loop(0, fold, one, 0)
+
     reach = ring.shape[2]
     W = (wide, wide_sem)
     R = (ring, ring_sem)
@@ -610,53 +644,57 @@
 
     @pl.when(diag)
     def _():
-        def mine(q):
-            for way in ("x", "z", "cut", "c"):
-                send(way, *R, own, q, ring_ref)
-
-        mine(0)
-        mine(1)
+        def mine(way, q):
+            send(way, *R, own, q, ring_ref)
+
+        for q in range(4):
+            mine("cut", q)
+            mine("x", q)
+            if q < 2:
+                mine("z", q)
+            mine("c", q)
         prepare()
         pass_on(*R, t_z, 0, "cut")
+        pass_on(*W, own, 0, "z")
+        pass_on(*R, t_z, 1, "cut")
+        pass_on(*W, t_x, 0, "z")
+        mine("z", 2)
+        mine("z", 3)
+        pass_on(*W, t_z, 0, "y")
         pass_on(*R, t_x, 0, "z")
-        pass_on(*W, own, 0, "z")
-        mine(2)
-        pass_on(*R, t_z, 1, "cut")
         pass_on(*R, t_x, 1, "z")
-        pass_on(*W, t_x, 0, "z")
-        pass_on(*W, t_z, 0, "y")
-        mine(3)
         pass_on(*W, t_z, 2, "x")
         pass_on(*W, t_d, 0, "y")
+        pass_on(*R, t_x, 2)
+        pass_on(*R, t_x, 3)
         pass_on(*R, t_z, 2, "x", "cut")
-        pass_on(*R, t_x, 2)
         pass_on(*W, own, 3, "x")
+        pass_on(*R, t_z, 3, "x", "cut")
         pass_on(*W, t_d, 2, "y")
-        pass_on(*R, t_z, 3, "x", "cut")
-        pass_on(*R, t_x, 3)
         load(*R, low, x, reach, ring_ref)
         mirrored(low, x)
         pass_on(*W, t_x, 1, "z")
         pass_on(*W, t_x, 3, "y")
+        energies()
+        load(*R, low, 1 - x, reach)
+        mirrored(low, 1 - x)
+        pass_on(*W, t_z, 3, "x")
+        pass_on(*W, t_d, 1, "y")
         load(*R, 1 - low, x, reach)
         mirrored(1 - low, x)
-        pass_on(*W, t_z, 3, "x")
-        pass_on(*W, t_d, 1, "y")
+        pass_on(*W, own, 1, "z")
         for q in range(4):
             pass_on(*R, t_d, q)
-        load(*R, low, 1 - x, reach)
-        mirrored(low, 1 - x)
-        pass_on(*W, own, 1, "z")
         pass_on(*W, t_d, 3, "y")
         load(*R, 1 - low, 1 - x, reach)
         mirrored(1 - low, 1 - x)
         pass_on(*W, own, 2, "x")
         load(*W, 1 - low, 1 - x, half)
         turned(1 - low, 1 - x)
+        load(*W, low, x, half)
+        turned(low, x)
         pass_on(*W, t_z, 1)
         pass_on(*W, t_x, 2)
-        load(*W, low, x, half)
-        turned(low, x)
         load(*W, 1 - low, x, half)
         turned(1 - low, x)
         load(*W, low, 1 - x, half)
@@ -665,8 +703,8 @@
 
     @pl.when(jnp.logical_not(diag))
     def _():
-        def mine(way, q):
-            send(way, *W, own, q, coeff_ref)
+        def mine(way, q, when=None):
+            send(way, *W, own, q, coeff_ref, when)
 
         mine("y", 0)
         mine("x", 0)
@@ -674,85 +712,70 @@
         mine("x", 1)
         mine("z", 3)
         mine("x", 2)
-        mine("z", 1)
+        mine("z", 1, end)
         for q in range(4):
             mine("c", q)
         pass_on(*W, t_x, 0, "y")
         pass_on(*W, t_z, 2, "y")
         mine("y", 3)
+        front = 1 - col
+        back = col
+        a_own, b_own = spot(front, x, core), spot(back, x, core)
+        a_far, b_far = spot(front, 1 - x, core), spot(back, 1 - x, core)
+
+        def inward(t, q):
+            arrive(*R, t, q)
+            send("x", *R, t, q)
+            send("z", *R, t, q, None, mid)
+            send("c", *R, t, q)
+
         prepare()
         pass_on(*W, t_x, 1, "y")
         pass_on(*W, t_z, 3, "y")
         mine("y", 1)
         mine("y", 2)
-        front = 1 - col
-        back = col
-        a_own, b_own = spot(front, x, core), spot(back, x, core)
-        a_far, b_far = spot(front, 1 - x, core), spot(back, 1 - x, core)
-
-        def inward(t, q):
-            arrive(*R, t, q)
-            send("x", *R, t, q)
-            copy = pltpu.make_async_remote_copy(
-                src_ref=part(ring, t, q),
-                dst_ref=part(ring, t, q),
-                send_sem=send_sem.at[len(sent)],
-                recv_sem=ring_sem.at[t, q],
-                device_id=targets["z"],
-                device_id_type=MESH,
-            )
-            sent.append((copy, True))
-
-            @pl.when(mid)
-            def _():
-                copy.start()
-
-            send("c", *R, t, q)
-
+        inward(a_own, 0)
+        inward(a_own, 1)
         load(*W, low, x, half, coeff_ref)
         plain(low, x)
-        inward(a_own, 0)
+        inward(a_own, 2)
+        inward(a_own, 3)
         pass_on(*W, t_x, 2)
+        pass_on(*W, t_z, 0)
+        inward(b_own, 0)
+        pass_on(*W, t_d, 0)
+        inward(b_own, 1)
+        energies()
+        for q in range(4):
+            pass_on(*R, a_far, q)
+        load(*R, front, x, reach)
+        mirrored(front, x)
+        pass_on(*W, t_d, 2)
+        inward(b_own, 2)
+        load(*R, front, 1 - x, reach)
+        mirrored(front, 1 - x)
+        inward(b_own, 3)
+        mine("z", 1, mid)
+        pass_on(*W, t_x, 3)
+        load(*W, low, 1 - x, half)
+        plain(low, 1 - x)
+        load(*R, back, x, reach)
+        mirrored(back, x)
+        pass_on(*W, t_d, 1)
+        for q in range(4):
+            pass_on(*R, b_far, q)
         pass_on(*W, t_z, 1)
-        inward(b_own, 0)
-        pass_on(*W, t_z, 0)
-        inward(a_own, 1)
-        inward(b_own, 1)
-        pass_on(*W, t_d, 0)
-        pass_on(*R, a_far, 0)
-        pass_on(*W, t_d, 2)
-        inward(a_own, 2)
-        pass_on(*R, b_far, 0)
-        inward(b_own, 2)
         load(*W, 1 - low, x, half)
         plain(1 - low, x)
-        pass_on(*W, t_x, 3)
-        pass_on(*R, a_far, 1)
-        inward(a_own, 3)
-        pass_on(*R, b_far, 1)
-        load(*W, low, 1 - x, half)
-        plain(low, 1 - x)
-        pass_on(*W, t_d, 1)
-        inward(b_own, 3)
-        pass_on(*R, a_far, 2)
-        load(*R, front, x, reach)
-        mirrored(front, x)
-        pass_on(*R, b_far, 2)
         pass_on(*W, t_d, 3)
-        load(*R, back, x, reach)
-        mirrored(back, x)
-        pass_on(*R, a_far, 3)
-        pass_on(*R, b_far, 3)
+        load(*R, back, 1 - x, reach)
+        mirrored(back, 1 - x)
         load(*W, 1 - low, 1 - x, half)
         plain(1 - low, 1 - x)
-        load(*R, front, 1 - x, reach)
-        mirrored(front, 1 - x)
-        load(*R, back, 1 - x, reach)
-        mirrored(back, 1 - x)
         settle()
 
 
-def gather_products(ham, tile_mask, coeff):
+def gather_products(ham, tile_mask, coeff, couple, occ_beta, energy_alpha, energy_beta):
     rows, strings = ham.shape
     half = coeff.shape[1]
     fold = half // rows
@@ -770,9 +793,10 @@
             jax.ShapeDtypeStruct((rows, half), jnp.float32),
             jax.ShapeDtypeStruct((fold, rows, half), jnp.bfloat16),
             jax.ShapeDtypeStruct((fold, rows, reach), jnp.bfloat16),
+            jax.ShapeDtypeStruct((rows, half), jnp.float32),
         ),
-        in_specs=[anywhere, vmem, anywhere, anywhere],
-        out_specs=(vmem, anywhere, anywhere),
+        in_specs=[anywhere, vmem, anywhere, anywhere, vmem, vmem, vmem, vmem],
+        out_specs=(vmem, anywhere, anywhere, vmem),
         scratch_shapes=[
             pltpu.VMEM((rows, strings), jnp.bfloat16),
             pltpu.VMEM((2 * rows, half), jnp.bfloat16),
@@ -785,7 +809,7 @@
             collective_id=9, has_side_effects=True, vmem_limit_bytes=50 * 1024 * 1024
         ),
         name="gather_products",
-    )(ham, tile_mask, coeff, ring)[0]
+    )(ham, tile_mask, coeff, ring, couple, occ_beta, energy_alpha[:, None], energy_beta[None, :])
 
 
 CHUNKS = 2
@@ -801,11 +825,14 @@
     occ_beta = lax.dynamic_slice_in_dim(occ_float, lax.axis_index("col") * tile_cols, tile_cols, 1)
     energy_alpha = jnp.dot(orbital_energy, occ_alpha, precision=HIGH)
     energy_beta = jnp.dot(orbital_energy, occ_beta, precision=HIGH)
-    coupling = jnp.dot(jnp.dot(occ_alpha.T, coulomb, precision=HIGH), occ_beta, precision=HIGH)
-    diagonal = energy_alpha[:, None] + energy_beta[None, :] + coupling
+    couple = jnp.dot(occ_alpha.T, coulomb, precision=HIGH)
     if direct:
-        result = turn(0, 1, [gather_products(ham, tile_mask, coeff)], [], coeff, diagonal, strings)
+        product, _, _, diagonal = gather_products(
+            ham, tile_mask, coeff, couple, occ_beta, energy_alpha, energy_beta
+        )
+        result = turn(0, 1, [product], [], coeff, diagonal, strings)
     else:
+        diagonal = energy_alpha[:, None] + energy_beta[None, :] + jnp.dot(couple, occ_beta, precision=HIGH)
         mask_cols = tile_mask.shape[1]
         block_size = strings // mask_cols
         mask_rows = tile_rows // block_size

time: 436 us -> 387 us (0.89)
  Pallas kernels: 408 us -> 367 us
  matrix products: 10.1 us -> 3.48 us
    pallas_call x1, Pallas kernels: 254 us -> 234 us  [gather_products(): pl.pallas_call(gather_kernel, out_shape=(jax.ShapeDtypeStruct((rows, half...]
    pallas_call x1, Pallas kernels: 153 us -> 133 us  [turn(): pl.pallas_call(functools.partial(turn_kernel, row_count, col_count, float...]
    dot_general x2 -> x1, matrix products: 9.67 us -> 0.6 us  [body(): couple = jnp.dot(occ_alpha.T, coulomb, precision=HIGH)]
where the time goes in v3:
time: 387 us; the launch traced here: 386 us
  Pallas kernels  367 us (95%)
  other arithmetic  11.7 us (3%)
    pallas_call x1, Pallas kernels, gather_products(): pl.pallas_call(gather_kernel, out_shape=(jax.ShapeDtypeStruct((rows, half...  234 us
    pallas_call x1, Pallas kernels, turn(): pl.pallas_call(functools.partial(turn_kernel, row_count, col_count, float...  133 us
    mul x1, other arithmetic, body(): correction = update * lax.rsqrt(sums[2] + 1e-06)  7.85 us

profile of v3, /device:TPU:0, one launch (start us, length us, event | category | flops | bytes accessed | tf_op | source)
XLA Modules:
  0.0 386.0 jit_solution(7922390354748345034)
XLA Ops:
  0.6 0.0 copy-start
  0.6 0.0 slice-start
  0.7 0.0 copy-start.3
  0.7 1.2 convert_element_type.3
  2.0 1.6 fusion.6.beta_ref
  3.6 1.3 convolution_bitcast_fusion.alpha_ref
  4.8 0.0 copy-done
  4.9 0.6 fusion.2.couple_ref
  5.5 0.0 copy-start.2
  5.5 0.0 slice-done
  5.5 0.0 copy-done.3
  5.5 1.4 fusion.ring_ref
  6.9 0.0 copy-done.2
  6.9 234.1 %gather_products.1 = (f32[512,4096]{1,0:T(8,128)}, bf16[8,512,4096]{2,1,0:T(8,128)(2,1)}, bf16[8,512,2560]{2,1,0:T(8,128)(2,1)}, f32[512,4096]{1,0:T(8,128)}) custom-call(bf16[512,8192]{1,0:T(8,128)(2,1)} %ham_ref.1, s32[16,256]{1,0:T(8,128)S(1)} %copy-done.2, bf16[512,4096]{1,0:T(8,128)(2,1)} %refs_2_.1, bf16[512,2560]{1,0:T(8,128)(2,1)S(1)} %fusion.ring_ref, ...), custom_call_target="tpu_custom_call" | custom-call | tf_op jit(solution)/shard_map/gather_products/pallas_call | solution.py:790
  241.0 133.1 %turn_0.1 = (f32[512,4096]{1,0:T(8,128)}, f32[3]{0:T(128)}) custom-call(f32[512,4096]{1,0:T(8,128)} %get-tuple-element.6.refs_0_, f32[512,4096]{1,0:T(8,128)} %get-tuple-element.7.refs_1_, bf16[512,4096]{1,0:T(8,128)(2,1)} %refs_2_.1), custom_call_target="tpu_custom_call" | custom-call | tf_op jit(solution)/shard_map/turn_0/pallas_call | solution.py:401
  374.1 1.4 fusion.9
  376.9 0.0 copy-start.1
  376.9 1.2 pad_maximum_fusion
  378.2 7.9 %broadcast_multiply_fusion = f32[512,4096]{1,0:T(8,128)} fusion(f32[512,4096]{1,0:T(8,128)} %get-tuple-element.8, f32[]{:T(128)} %bitcast.5), kind=kLoop, calls=%fused_computation.2 | loop fusion | flops 2097152 | bytes 16777220 | tf_op jit(solution)/shard_map/mul | solution.py:854
  386.0 0.0 copy-done.1
  (1 shorter events, 0.0 us)
Async XLA Ops:
  0.6 4.2 %copy-start = (f32[16,16]{1,0:T(8,128)S(1)}, f32[16,16]{1,0:T(8,128)}, u32[]{:S(2)}) copy-start(f32[16,16]{1,0:T(8,128)} %param.11) | copy-start | bytes 3076
  0.6 4.8 %slice-start = ((bf16[512,4096]{1,0:T(8,128)(2,1)}), bf16[512,2048]{1,0:T(8,128)(2,1)S(1)}, s32[]{:S(2)}) async-start(bf16[512,4096]{1,0:T(8,128)(2,1)} %refs_2_.1), calls=%async_computation | async-start | bytes 4194304 | tf_op jit(solution)/shard_map/slice | solution.py:785
  0.7 4.8 %copy-start.3 = (bf16[512,4096]{1,0:T(8,128)(2,1)S(1)}, bf16[512,4096]{1,0:T(8,128)(2,1)}, u32[]{:S(2)}) copy-start(bf16[512,4096]{1,0:T(8,128)(2,1)} %refs_2_.1) | copy-start | bytes 12582916
  5.5 1.4 copy-start.2
  376.9 9.1 %copy-start.1 = (f32[16,16]{1,0:T(8,128)S(1)}, f32[16,16]{1,0:T(8,128)}, u32[]{:S(2)}) copy-start(f32[16,16]{1,0:T(8,128)} %param.11) | copy-start | bytes 3076

commit v4 on v3

--- a/solution.py
+++ b/solution.py
@@ -405,31 +405,50 @@
         out_specs=out_specs,
         scratch_shapes=scratch,
         compiler_params=pltpu.CompilerParams(
-            collective_id=chunk, has_side_effects=True, vmem_limit_bytes=(60 if last else 24) * 1024 * 1024
+            collective_id=chunk,
+            has_side_effects=True,
+            vmem_limit_bytes=(24 if not last else 60 if chunks == 1 else 60) * 1024 * 1024,
         ),
         name=f"turn_{chunk}",
     )(*operands)
 
 
-def gather_kernel(
+def step_kernel(
+    total,
     ham_ref,
     mask_ref,
     coeff_ref,
     ring_ref,
-    couple_ref,
     occ_ref,
-    alpha_ref,
-    beta_ref,
-    acc_ref,
+    level_ref,
+    coulomb_ref,
+    out_ref,
     wide,
     ring,
-    diagonal_ref,
+    stats_ref,
+    acc_ref,
     m_ref,
     buf,
+    c_ref,
+    packed,
+    relay_a,
+    relay_b,
+    recv,
+    mine_sums,
+    sums,
     load_sem,
     send_sem,
     wide_sem,
     ring_sem,
+    own_send,
+    recv_sem,
+    arrive_a,
+    arrive_b,
+    send_a,
+    send_b,
+    self_sem,
+    sum_send,
+    sum_recv,
 ):
     rows, strings = ham_ref.shape
     half = coeff_ref.shape[1]
@@ -457,11 +476,33 @@
 
     ham_load = pltpu.make_async_copy(ham_ref, m_ref, load_sem.at[0])
     ham_load.start()
+    coeff_load = pltpu.make_async_copy(coeff_ref, c_ref, load_sem.at[3])
+    coeff_load.start()
+
+    count = sums.shape[1]
+    me = row * 2 + col
+
+    def remote(src, dst, send_one, arrive_one, to_row, to_col):
+        return pltpu.make_async_remote_copy(
+            src_ref=src,
+            dst_ref=dst,
+            send_sem=send_one,
+            recv_sem=arrive_one,
+            device_id=(to_row, to_col),
+            device_id_type=MESH,
+        )
 
     barrier = pltpu.get_barrier_semaphore()
-    for target in targets.values():
-        pl.semaphore_signal(barrier, inc=1, device_id=target, device_id_type=MESH)
-    pl.semaphore_wait(barrier, len(targets))
+
+    def greet(d, carry):
+        other = lax.rem(me + d, count)
+        pl.semaphore_signal(
+            barrier, inc=1, device_id=(lax.div(other, 2), lax.rem(other, 2)), device_id_type=MESH
+        )
+        return carry
+
+    lax.fori_loop(1, count, greet, 0)
+    pl.semaphore_wait(barrier, count - 1)
 
     def spot(l, a, k):
         return (l * 2 + a) * 2 + k
@@ -624,11 +665,16 @@
         lax.fori_loop(0, strings // step, one, 0)
 
     def energies():
+        alpha = occ_ref[:, block(row)].astype(jnp.float32).T
+        couple = jnp.dot(alpha, coulomb_ref[...], precision=HIGH, preferred_element_type=jnp.float32)
+        energy = jnp.sum(alpha * level_ref[...], axis=1, keepdims=True)
+
         def one(n, carry):
-            diagonal_ref[:, block(n)] = (
-                jnp.dot(couple_ref[...], occ_ref[:, block(n)], precision=HIGH, preferred_element_type=jnp.float32)
-                + alpha_ref[...]
-                + beta_ref[:, block(n)]
+            beta = occ_ref[:, block(near + n)].astype(jnp.float32)
+            out_ref[:, block(n)] = (
+                jnp.dot(couple, beta, precision=HIGH, preferred_element_type=jnp.float32)
+                + energy
+                + jnp.dot(level_ref[...], beta, precision=HIGH, preferred_element_type=jnp.float32)
             )
             return carry
 
@@ -774,42 +820,263 @@
         plain(1 - low, 1 - x)
         settle()
 
-
-def gather_products(ham, tile_mask, coeff, couple, occ_beta, energy_alpha, energy_beta):
+    place = lax.rem(row, fold)
+    far_col = 1 - col
+    piece_half = rows // 2
+
+    def own_direct(k):
+        s = lax.rem(place + k, fold)
+        return [
+            remote(packed.at[s, h], recv.at[place, h], own_send.at[s, h], recv_sem.at[place, h], near + s, col)
+            for h in range(2)
+        ]
+
+    def own_relayed(k):
+        s = lax.rem(place + k, fold)
+        return [
+            remote(packed.at[s, 0], relay_a.at[s], own_send.at[s, 0], arrive_a.at[s], row, far_col),
+            remote(packed.at[s, 1], relay_b.at[place], own_send.at[s, 1], arrive_b.at[place], near + s, col),
+        ]
+
+    def own_local():
+        return [pltpu.make_async_copy(packed.at[place, h], recv.at[place, h], self_sem.at[h]) for h in range(2)]
+
+    def pack(k):
+        s = lax.rem(place + k, fold)
+        for h in range(2):
+            peak = jnp.max(jnp.abs(acc_ref[pl.ds(h * piece_half, piece_half), block(s)]), axis=0, keepdims=True)
+            code = jnp.floor(jnp.log2(jnp.maximum(peak, 1e-30)) * 128.0) + 2.0
+            grow = jnp.exp2(code * (-1.0 / 128.0)) * 32767.0
+            packed[s, h, pl.ds(piece_half, 16)] = (
+                jnp.broadcast_to(code, (16, rows)).astype(jnp.int32).astype(jnp.int16)
+            )
+            for r in range(0, piece_half, 64):
+                value = acc_ref[pl.ds(h * piece_half + r, 64), block(s)] * grow
+                packed[s, h, pl.ds(r, 64)] = jnp.floor(value + 0.5).astype(jnp.int32).astype(jnp.int16)
+
+    def exchange(phase, start):
+        def one(d, carry):
+            other = lax.rem(me + d, count)
+            copy = remote(
+                mine_sums.at[phase],
+                sums.at[phase, me],
+                sum_send.at[phase, d],
+                sum_recv.at[phase, me],
+                lax.div(other, 2),
+                lax.rem(other, 2),
+            )
+            if start:
+                copy.start()
+            else:
+                copy.wait_send()
+            return carry
+
+        lax.fori_loop(1, count, one, 0)
+
+    def gather_sums(phase):
+        def one(d, carry):
+            other = lax.rem(me + d, count)
+            view = sums.at[phase, other]
+            pltpu.make_async_copy(view, view, sum_recv.at[phase, other]).wait()
+            return carry
+
+        lax.fori_loop(1, count, one, 0)
+        sums[phase, pl.ds(me, 1)] = mine_sums[pl.ds(phase, 1)]
+        every = jnp.sum(sums[phase], axis=0)
+        return jnp.sum(every[0:8]), jnp.sum(every[8:16])
+
+    def fold_sum(v):
+        out = v[:, 0:128]
+        for q in range(1, v.shape[1] // 128):
+            out = out + v[:, q * 128 : (q + 1) * 128]
+        return jnp.sum(out.reshape(v.shape[0] // 8, 8, 128), axis=0)
+
+    def launch(k, carry):
+        pack(k)
+
+        @pl.when(jnp.logical_not(diag))
+        def _():
+            for copy in own_relayed(k):
+                copy.start()
+
+        @pl.when(jnp.logical_and(diag, k > 0))
+        def _():
+            for copy in own_direct(k):
+                copy.start()
+
+        return carry
+
+    lax.fori_loop(0, fold, launch, 0)
+
+    zero = jnp.zeros((8, 128), jnp.float32)
+    step_rows = min(32, rows)
+    coeff_load.wait()
+
+    def early(r, carry):
+        band = pl.ds(pl.multiple_of(r * step_rows, step_rows), step_rows)
+        c = c_ref[band, :].astype(jnp.float32)
+        return carry[0] + fold_sum(c * acc_ref[band, :]), carry[1] + fold_sum(c * c)
+
+    proj, weight = lax.fori_loop(0, rows // step_rows, early, (zero, zero))
+    mine_sums[0, 0:8] = proj
+    mine_sums[0, 8:16] = weight
+    exchange(0, True)
+
+    @pl.when(diag)
+    def _():
+        for copy in own_local():
+            copy.start()
+        for copy in own_local():
+            copy.wait()
+
+    def relay_first(t):
+        s = lax.rem(place + t, fold)
+        return s, remote(
+            relay_a.at[s], recv.at[place, 0], send_a.at[t], recv_sem.at[place, 0], far_col * fold + s, col
+        )
+
+    def relay_second(t):
+        far = lax.rem(place - t + fold, fold)
+        return far, remote(relay_b.at[far], recv.at[far, 1], send_b.at[t], recv_sem.at[far, 1], row, far_col)
+
+    @pl.when(diag)
+    def _():
+        def relay(t, carry):
+            s, copy = relay_first(t)
+            pltpu.make_async_copy(relay_a.at[s], relay_a.at[s], arrive_a.at[s]).wait()
+            copy.start()
+            far, copy = relay_second(t)
+            pltpu.make_async_copy(relay_b.at[far], relay_b.at[far], arrive_b.at[far]).wait()
+            copy.start()
+            return carry
+
+        lax.fori_loop(0, fold, relay, 0)
+
+    def await_piece(k):
+        s = lax.rem(place - k + fold, fold)
+
+        @pl.when(jnp.logical_not(jnp.logical_and(diag, k == 0)))
+        def _():
+            for h in range(2):
+                pltpu.make_async_copy(recv.at[s, h], recv.at[s, h], recv_sem.at[s, h]).wait()
+
+    proj, weight = gather_sums(0)
+    theta = 2.0 * proj / weight
+    piece = min(128, rows)
+
+    def finish(k, carry):
+        s = lax.rem(place - k + fold, fold)
+        await_piece(k)
+
+        def part_of(r, inner):
+            squares, spread = inner
+            band = pl.ds(pl.multiple_of(r * piece, piece), piece)
+            for h in range(2):
+                cols = pl.ds(pl.multiple_of(s * rows + h * piece_half, piece_half), piece_half)
+                code = recv[s, h, pl.ds(piece_half, 16), band].astype(jnp.int32).astype(jnp.float32)[0:1]
+                shrink = jnp.exp2(code * (1.0 / 128.0)) * (1.0 / 32767.0)
+                value = recv[s, h, pl.ds(0, piece_half), band].astype(jnp.int32).astype(jnp.float32)
+                sigma = acc_ref[band, cols] + (value * shrink).T
+                residual = sigma - theta * c_ref[band, cols].astype(jnp.float32)
+                update = residual / jnp.maximum(jnp.abs(out_ref[band, cols] - theta), 1.0)
+                out_ref[band, cols] = update
+                squares = squares + fold_sum(residual * residual)
+                spread = spread + fold_sum(update * update)
+            return squares, spread
+
+        return lax.fori_loop(0, rows // piece, part_of, carry)
+
+    squares, spread = lax.fori_loop(0, fold, finish, (zero, zero))
+    mine_sums[1, 0:8] = squares
+    mine_sums[1, 8:16] = spread
+    exchange(1, True)
+    squares, spread = gather_sums(1)
+    stats_ref[0] = theta
+    stats_ref[1] = squares / total
+    stats_ref[2] = spread / total
+
+    exchange(0, False)
+    exchange(1, False)
+
+    @pl.when(diag)
+    def _():
+        def done(t, carry):
+            @pl.when(t > 0)
+            def _():
+                for copy in own_direct(t):
+                    copy.wait_send()
+
+            relay_first(t)[1].wait_send()
+            relay_second(t)[1].wait_send()
+            return carry
+
+        lax.fori_loop(0, fold, done, 0)
+
+    @pl.when(jnp.logical_not(diag))
+    def _():
+        def done(t, carry):
+            for copy in own_relayed(t):
+                copy.wait_send()
+            return carry
+
+        lax.fori_loop(0, fold, done, 0)
+
+
+def whole_step(ham, tile_mask, coeff, occupation, orbital_energy, coulomb):
     rows, strings = ham.shape
     half = coeff.shape[1]
     fold = half // rows
+    count = lax.axis_size("row") * lax.axis_size("col")
     row = lax.axis_index("row")
     reach = (fold // 2 + 1) * rows
     start = jnp.where(lax.div(row, fold) == lax.axis_index("col"), lax.rem(row, fold) * rows, 0)
     doubled = jnp.concatenate([coeff, coeff[:, : reach - rows]], axis=1)
     ring = lax.dynamic_slice(doubled, (0, start), (rows, reach))
+    tall = rows // 2 + 16
     anywhere = pl.BlockSpec(memory_space=pl.ANY)
     vmem = pl.BlockSpec(memory_space=pltpu.VMEM)
     dma = pltpu.SemaphoreType.DMA
-    return pl.pallas_call(
-        gather_kernel,
+    update, _, _, sums = pl.pallas_call(
+        functools.partial(step_kernel, float(strings) * float(strings)),
         out_shape=(
             jax.ShapeDtypeStruct((rows, half), jnp.float32),
             jax.ShapeDtypeStruct((fold, rows, half), jnp.bfloat16),
             jax.ShapeDtypeStruct((fold, rows, reach), jnp.bfloat16),
-            jax.ShapeDtypeStruct((rows, half), jnp.float32),
+            jax.ShapeDtypeStruct((3,), jnp.float32),
         ),
-        in_specs=[anywhere, vmem, anywhere, anywhere, vmem, vmem, vmem, vmem],
-        out_specs=(vmem, anywhere, anywhere, vmem),
+        in_specs=[anywhere, vmem, anywhere, anywhere, vmem, vmem, vmem],
+        out_specs=(vmem, anywhere, anywhere, pl.BlockSpec(memory_space=pltpu.SMEM)),
         scratch_shapes=[
+            pltpu.VMEM((rows, half), jnp.float32),
             pltpu.VMEM((rows, strings), jnp.bfloat16),
             pltpu.VMEM((2 * rows, half), jnp.bfloat16),
-            dma((3,)),
+            pltpu.VMEM((rows, half), jnp.bfloat16),
+            pltpu.VMEM((fold, 2, tall, rows), jnp.int16),
+            pltpu.VMEM((fold, tall, rows), jnp.int16),
+            pltpu.VMEM((fold, tall, rows), jnp.int16),
+            pltpu.VMEM((fold, 2, tall, rows), jnp.int16),
+            pltpu.VMEM((2, 16, 128), jnp.float32),
+            pltpu.VMEM((2, count, 16, 128), jnp.float32),
+            dma((4,)),
             dma((80,)),
             dma((fold, 4)),
             dma((fold, 4)),
+            dma((fold, 2)),
+            dma((fold, 2)),
+            dma((fold,)),
+            dma((fold,)),
+            dma((fold,)),
+            dma((fold,)),
+            dma((2,)),
+            dma((2, count)),
+            dma((2, count)),
         ],
         compiler_params=pltpu.CompilerParams(
-            collective_id=9, has_side_effects=True, vmem_limit_bytes=50 * 1024 * 1024
+            collective_id=9, has_side_effects=True, vmem_limit_bytes=62 * 1024 * 1024
         ),
-        name="gather_products",
-    )(ham, tile_mask, coeff, ring, couple, occ_beta, energy_alpha[:, None], energy_beta[None, :])
+        name="whole_step",
+    )(ham, tile_mask, coeff, ring, occupation, orbital_energy[None, :], coulomb)
+    return update, sums
 
 
 CHUNKS = 2
@@ -820,18 +1087,15 @@
     tile_cols = coeff.shape[1]
     fold = tile_cols // tile_rows
     direct = lax.axis_size("col") == 2 and lax.axis_size("row") == 16
-    occ_float = occupation.astype(jnp.float32)
-    occ_alpha = lax.dynamic_slice_in_dim(occ_float, lax.axis_index("row") * tile_rows, tile_rows, 1)
-    occ_beta = lax.dynamic_slice_in_dim(occ_float, lax.axis_index("col") * tile_cols, tile_cols, 1)
-    energy_alpha = jnp.dot(orbital_energy, occ_alpha, precision=HIGH)
-    energy_beta = jnp.dot(orbital_energy, occ_beta, precision=HIGH)
-    couple = jnp.dot(occ_alpha.T, coulomb, precision=HIGH)
     if direct:
-        product, _, _, diagonal = gather_products(
-            ham, tile_mask, coeff, couple, occ_beta, energy_alpha, energy_beta
-        )
-        result = turn(0, 1, [product], [], coeff, diagonal, strings)
+        result = whole_step(ham, tile_mask, coeff, occupation, orbital_energy, coulomb)
     else:
+        occ_float = occupation.astype(jnp.float32)
+        occ_alpha = lax.dynamic_slice_in_dim(occ_float, lax.axis_index("row") * tile_rows, tile_rows, 1)
+        occ_beta = lax.dynamic_slice_in_dim(occ_float, lax.axis_index("col") * tile_cols, tile_cols, 1)
+        energy_alpha = jnp.dot(orbital_energy, occ_alpha, precision=HIGH)
+        energy_beta = jnp.dot(orbital_energy, occ_beta, precision=HIGH)
+        couple = jnp.dot(occ_alpha.T, coulomb, precision=HIGH)
         diagonal = energy_alpha[:, None] + energy_beta[None, :] + jnp.dot(couple, occ_beta, precision=HIGH)
         mask_cols = tile_mask.shape[1]
         block_size = strings // mask_cols

time: 387 us -> 399 us (1.031)
  Pallas kernels: 367 us -> 381 us
    pallas_call x2 -> x1, Pallas kernels: 367 us -> 381 us  [whole_step(): pl.pallas_call(functools.partial(step_kernel, float(strings) * float(stri...]
where the time goes in v4:
time: 399 us
  Pallas kernels  381 us (95%)
  other arithmetic  13.4 us (3%)
    pallas_call x1, Pallas kernels, whole_step(): pl.pallas_call(functools.partial(step_kernel, float(strings) * float(stri...  381 us

profile of v4, /device:TPU:0, one launch (start us, length us, event | category | flops | bytes accessed | tf_op | source)
XLA Modules:
  0.0 399.1 jit_solution(5697453662704750110)
XLA Ops:
  0.6 0.0 slice-start
  0.7 1.6 slice-done
  2.2 4.3 %fusion.ring_ref = bf16[512,2560]{1,0:T(8,128)(2,1)} fusion(s32[]{:T(128)S(6)} %select_n.8, bf16[512,4096]{1,0:T(8,128)(2,1)} %coeff_ref.1, bf16[512,2048]{1,0:T(8,128)(2,1)S(1)} %slice-done), kind=kLoop, calls=%fused_computation.3 | loop fusion | flops 5242880 | bytes 8912900 | tf_op jit(solution)/shard_map/concatenate | solution.py:1033
  6.5 380.8 %whole_step.1 = (f32[512,4096]{1,0:T(8,128)}, bf16[8,512,4096]{2,1,0:T(8,128)(2,1)}, bf16[8,512,2560]{2,1,0:T(8,128)(2,1)}, f32[3]{0:T(128)}) custom-call(bf16[512,8192]{1,0:T(8,128)(2,1)} %ham_ref.1, s32[16,256]{1,0:T(8,128)} %mask_ref.1, bf16[512,4096]{1,0:T(8,128)(2,1)} %coeff_ref.1, bf16[512,2560]{1,0:T(8,128)(2,1)} %fusion.ring_ref, ...), custom_call_target="tpu_custom_call" | custom-call | tf_op jit(solution)/shard_map/whole_step/pallas_call | solution.py:1039
  387.3 1.3 fusion.1
  390.0 1.2 pad_maximum_fusion
  391.2 7.9 %broadcast_multiply_fusion = f32[512,4096]{1,0:T(8,128)} fusion(f32[512,4096]{1,0:T(8,128)} %get-tuple-element.4, f32[]{:T(128)} %bitcast.1), kind=kLoop, calls=%fused_computation.2 | loop fusion | flops 2097152 | bytes 16777220 | tf_op jit(solution)/shard_map/mul | solution.py:1118
Async XLA Ops:
  0.6 1.6 slice-start

commit v5 on v4

--- a/solution.py
+++ b/solution.py
@@ -418,7 +418,6 @@
     ham_ref,
     mask_ref,
     coeff_ref,
-    ring_ref,
     occ_ref,
     level_ref,
     coulomb_ref,
@@ -429,6 +428,7 @@
     acc_ref,
     m_ref,
     buf,
+    ring_ref,
     c_ref,
     packed,
     relay_a,
@@ -449,6 +449,7 @@
     self_sem,
     sum_send,
     sum_recv,
+    ring_load,
 ):
     rows, strings = ham_ref.shape
     half = coeff_ref.shape[1]
@@ -479,6 +480,20 @@
     coeff_load = pltpu.make_async_copy(coeff_ref, c_ref, load_sem.at[3])
     coeff_load.start()
 
+    ring_loads = [
+        pltpu.make_async_copy(
+            coeff_ref.at[:, pl.ds(pl.multiple_of(lax.rem(row + d, fold) * rows, rows), rows)],
+            ring_ref.at[:, pl.ds(d * rows, rows)],
+            ring_load.at[d],
+        )
+        for d in range(fold // 2 + 1)
+    ]
+
+    @pl.when(diag)
+    def _():
+        for copy in ring_loads:
+            copy.start()
+
     count = sums.shape[1]
     me = row * 2 + col
 
@@ -693,6 +708,8 @@
         def mine(way, q):
             send(way, *R, own, q, ring_ref)
 
+        for copy in ring_loads:
+            copy.wait()
         for q in range(4):
             mine("cut", q)
             mine("x", q)
@@ -891,7 +908,37 @@
             out = out + v[:, q * 128 : (q + 1) * 128]
         return jnp.sum(out.reshape(v.shape[0] // 8, 8, 128), axis=0)
 
+    zero = jnp.zeros((8, 128), jnp.float32)
+    step_rows = min(32, rows)
+    coeff_load.wait()
+
+    def early(r, carry):
+        band = pl.ds(pl.multiple_of(r * step_rows, step_rows), step_rows)
+        c = c_ref[band, :].astype(jnp.float32)
+        return carry[0] + fold_sum(c * acc_ref[band, :]), carry[1] + fold_sum(c * c)
+
+    proj, weight = lax.fori_loop(0, rows // step_rows, early, (zero, zero))
+    mine_sums[0, 0:8] = proj
+    mine_sums[0, 8:16] = weight
+    exchange(0, True)
+
+    def relay_first(t):
+        s = lax.rem(place + t, fold)
+        return s, remote(
+            relay_a.at[s], recv.at[place, 0], send_a.at[t], recv_sem.at[place, 0], far_col * fold + s, col
+        )
+
+    def relay_second(t):
+        far = lax.rem(place - t + fold, fold)
+        return far, remote(relay_b.at[far], recv.at[far, 1], send_b.at[t], recv_sem.at[far, 1], row, far_col)
+
     def launch(k, carry):
+        @pl.when(diag)
+        def _():
+            s, copy = relay_first(k)
+            pltpu.make_async_copy(relay_a.at[s], relay_a.at[s], arrive_a.at[s]).wait()
+            copy.start()
+
         pack(k)
 
         @pl.when(jnp.logical_not(diag))
@@ -907,20 +954,6 @@
         return carry
 
     lax.fori_loop(0, fold, launch, 0)
-
-    zero = jnp.zeros((8, 128), jnp.float32)
-    step_rows = min(32, rows)
-    coeff_load.wait()
-
-    def early(r, carry):
-        band = pl.ds(pl.multiple_of(r * step_rows, step_rows), step_rows)
-        c = c_ref[band, :].astype(jnp.float32)
-        return carry[0] + fold_sum(c * acc_ref[band, :]), carry[1] + fold_sum(c * c)
-
-    proj, weight = lax.fori_loop(0, rows // step_rows, early, (zero, zero))
-    mine_sums[0, 0:8] = proj
-    mine_sums[0, 8:16] = weight
-    exchange(0, True)
 
     @pl.when(diag)
     def _():
@@ -929,22 +962,9 @@
         for copy in own_local():
             copy.wait()
 
-    def relay_first(t):
-        s = lax.rem(place + t, fold)
-        return s, remote(
-            relay_a.at[s], recv.at[place, 0], send_a.at[t], recv_sem.at[place, 0], far_col * fold + s, col
-        )
-
-    def relay_second(t):
-        far = lax.rem(place - t + fold, fold)
-        return far, remote(relay_b.at[far], recv.at[far, 1], send_b.at[t], recv_sem.at[far, 1], row, far_col)
-
     @pl.when(diag)
     def _():
         def relay(t, carry):
-            s, copy = relay_first(t)
-            pltpu.make_async_copy(relay_a.at[s], relay_a.at[s], arrive_a.at[s]).wait()
-            copy.start()
             far, copy = relay_second(t)
             pltpu.make_async_copy(relay_b.at[far], relay_b.at[far], arrive_b.at[far]).wait()
             copy.start()
@@ -1027,11 +1047,7 @@
     half = coeff.shape[1]
     fold = half // rows
     count = lax.axis_size("row") * lax.axis_size("col")
-    row = lax.axis_index("row")
     reach = (fold // 2 + 1) * rows
-    start = jnp.where(lax.div(row, fold) == lax.axis_index("col"), lax.rem(row, fold) * rows, 0)
-    doubled = jnp.concatenate([coeff, coeff[:, : reach - rows]], axis=1)
-    ring = lax.dynamic_slice(doubled, (0, start), (rows, reach))
     tall = rows // 2 + 16
     anywhere = pl.BlockSpec(memory_space=pl.ANY)
     vmem = pl.BlockSpec(memory_space=pltpu.VMEM)
@@ -1044,12 +1060,13 @@
             jax.ShapeDtypeStruct((fold, rows, reach), jnp.bfloat16),
             jax.ShapeDtypeStruct((3,), jnp.float32),
         ),
-        in_specs=[anywhere, vmem, anywhere, anywhere, vmem, vmem, vmem],
+        in_specs=[anywhere, vmem, anywhere, vmem, vmem, vmem],
         out_specs=(vmem, anywhere, anywhere, pl.BlockSpec(memory_space=pltpu.SMEM)),
         scratch_shapes=[
             pltpu.VMEM((rows, half), jnp.float32),
             pltpu.VMEM((rows, strings), jnp.bfloat16),
             pltpu.VMEM((2 * rows, half), jnp.bfloat16),
+            pltpu.VMEM((rows, reach), jnp.bfloat16),
             pltpu.VMEM((rows, half), jnp.bfloat16),
             pltpu.VMEM((fold, 2, tall, rows), jnp.int16),
             pltpu.VMEM((fold, tall, rows), jnp.int16),
@@ -1070,12 +1087,13 @@
             dma((2,)),
             dma((2, count)),
             dma((2, count)),
+            dma((fold // 2 + 1,)),
         ],
         compiler_params=pltpu.CompilerParams(
             collective_id=9, has_side_effects=True, vmem_limit_bytes=62 * 1024 * 1024
         ),
         name="whole_step",
-    )(ham, tile_mask, coeff, ring, occupation, orbital_energy[None, :], coulomb)
+    )(ham, tile_mask, coeff, occupation, orbital_energy[None, :], coulomb)
     return update, sums
 
 

time: 399 us -> 378 us (0.947)
  Pallas kernels: 381 us -> 365 us
  other arithmetic: 13.4 us -> 9.08 us
    pallas_call x1, Pallas kernels: 381 us -> 365 us  [whole_step(): pl.pallas_call(functools.partial(step_kernel, float(strings) * float(stri...]
    concatenate x1 -> x0, other arithmetic: 4.3 us -> none  [whole_step(): doubled = jnp.concatenate([coeff, coeff[:, :reach - rows]], axis=1)]
where the time goes in v5:
time: 378 us
  Pallas kernels  365 us (97%)
  other arithmetic  9.08 us (2%)
    pallas_call x1, Pallas kernels, whole_step(): pl.pallas_call(functools.partial(step_kernel, float(strings) * float(stri...  365 us
    mul x1, other arithmetic, body(): correction = update * lax.rsqrt(sums[2] + 1e-06)  7.85 us

profile of v5, /device:TPU:0, one launch (start us, length us, event | category | flops | bytes accessed | tf_op | source)
XLA Modules:
  0.0 377.5 jit_solution(17949640616478777103)
XLA Ops:
  0.6 365.0 %whole_step.1 = (f32[512,4096]{1,0:T(8,128)}, bf16[8,512,4096]{2,1,0:T(8,128)(2,1)}, bf16[8,512,2560]{2,1,0:T(8,128)(2,1)}, f32[3]{0:T(128)}) custom-call(bf16[512,8192]{1,0:T(8,128)(2,1)} %ham_ref.1, s32[16,256]{1,0:T(8,128)} %mask_ref.1, bf16[512,4096]{1,0:T(8,128)(2,1)} %coeff_ref.1, s32[16,8192]{1,0:T(8,128)} %occ_ref.1, f32[1,16]{1,0:T(1,128)} %bitcast.2, ...), custom_call_target="tpu_custom_call" | custom-call | tf_op jit(solution)/shard_map/whole_step/pallas_call | solution.py:1055
  365.7 1.4 fusion
  368.4 1.2 pad_maximum_fusion
  369.7 7.9 %broadcast_multiply_fusion = f32[512,4096]{1,0:T(8,128)} fusion(f32[512,4096]{1,0:T(8,128)} %get-tuple-element.4, f32[]{:T(128)} %bitcast.1), kind=kLoop, calls=%fused_computation | loop fusion | flops 2097152 | bytes 16777220 | tf_op jit(solution)/shard_map/mul | solution.py:1136

commit v6 on v5

--- a/solution.py
+++ b/solution.py
@@ -425,6 +425,7 @@
     wide,
     ring,
     stats_ref,
+    scale_ref,
     acc_ref,
     m_ref,
     buf,
@@ -522,21 +523,29 @@
     def spot(l, a, k):
         return (l * 2 + a) * 2 + k
 
-    def part(ref, t, q):
-        return ref.at[t, pl.ds(q * quarter, quarter)]
+    def cuts(ref, q):
+        return 2 if ref is wide and q in (1, 2) else 1
+
+    def span(ref, q, sub):
+        size = quarter // cuts(ref, q)
+        return pl.ds(q * quarter + sub * size, size)
 
     end = jnp.logical_not(mid)
     sent = []
 
-    def send(way, ref, sems, t, q, own=None, when=None):
-        src = part(ref, t, q) if own is None else own.at[pl.ds(q * quarter, quarter)]
+    def send(way, ref, sems, t, q, own=None, when=None, sub=None):
+        if sub is None:
+            for one in range(cuts(ref, q)):
+                send(way, ref, sems, t, q, own, when, one)
+            return
+        src = ref.at[t] if own is None else own
         if way == "cut":
             when = mid
         copy = pltpu.make_async_remote_copy(
-            src_ref=src,
-            dst_ref=part(ref, t, q),
+            src_ref=src.at[span(ref, q, sub)],
+            dst_ref=ref.at[t, span(ref, q, sub)],
             send_sem=send_sem.at[len(sent)],
-            recv_sem=sems.at[t, q],
+            recv_sem=sems.at[t, q, sub],
             device_id=targets[way],
             device_id_type=MESH,
         )
@@ -561,33 +570,43 @@
 
         sent.clear()
 
-    def arrive(ref, sems, t, q):
-        view = part(ref, t, q)
-        pltpu.make_async_copy(view, view, sems.at[t, q]).wait()
+    def arrive(ref, sems, t, q, sub):
+        view = ref.at[t, span(ref, q, sub)]
+        pltpu.make_async_copy(view, view, sems.at[t, q, sub]).wait()
 
     def pass_on(ref, sems, t, q, *ways):
-        arrive(ref, sems, t, q)
-        for way in ways:
-            send(way, ref, sems, t, q)
-        send("c", ref, sems, t, q)
-
-    def load(ref, sems, l, a, width, own=None):
+        for sub in range(cuts(ref, q)):
+            arrive(ref, sems, t, q, sub)
+            for way in ways:
+                send(way, ref, sems, t, q, sub=sub)
+            send("c", ref, sems, t, q, sub=sub)
+
+    short = rows // 2
+
+    def load(ref, sems, l, a, width, own=None, side=None):
         mine, other = spot(l, a, core), spot(l, a, 1 - core)
-        for q in range(4):
-            arrive(ref, sems, other, q)
+        first_row, size = (0, rows) if side is None else (side * short, short)
+        for q in range(first_row // quarter, (first_row + size) // quarter):
+            for sub in range(cuts(ref, q)):
+                arrive(ref, sems, other, q, sub)
         src = ref.at[mine] if own is None else own
-        first = pltpu.make_async_copy(
-            src, buf.at[pl.ds(pl.multiple_of(core * rows, rows), rows), pl.ds(0, width)], load_sem.at[1]
-        )
-        second = pltpu.make_async_copy(
-            ref.at[other],
-            buf.at[pl.ds(pl.multiple_of((1 - core) * rows, rows), rows), pl.ds(0, width)],
-            load_sem.at[2],
-        )
-        first.start()
-        second.start()
-        first.wait()
-        second.wait()
+        copies = [
+            pltpu.make_async_copy(
+                one.at[pl.ds(first_row, size)],
+                buf.at[pl.ds(pl.multiple_of(k * rows + first_row, short), size), pl.ds(0, width)],
+                load_sem.at[n],
+            )
+            for n, one, k in ((1, src, core), (2, ref.at[other], 1 - core))
+        ]
+        for copy in copies:
+            copy.start()
+        for copy in copies:
+            copy.wait()
+
+    def piece_of(n, side):
+        if side is None:
+            return block(n)
+        return pl.ds(pl.multiple_of(n * rows + side * short, short), short)
 
     def block(n):
         return pl.ds(pl.multiple_of(n * rows, rows), rows)
@@ -595,35 +614,46 @@
     near = col * fold
     away = (1 - col) * fold
 
-    def plain(l, a):
+    def plain(l, a, side=None):
         base = spot(l, a, 0)
-        left = pl.ds(pl.multiple_of((away + base) * rows, rows), 2 * rows)
 
         def one(n, carry):
-            acc_ref[:, block(n)] += jnp.dot(m_ref[:, left], buf[:, block(n)], preferred_element_type=jnp.float32)
+            if side is None:
+                left = pl.ds(pl.multiple_of((away + base) * rows, rows), 2 * rows)
+                total = jnp.dot(m_ref[:, left], buf[:, block(n)], preferred_element_type=jnp.float32)
+            else:
+                total = sum(
+                    jnp.dot(
+                        m_ref[:, piece_of(away + base + k, side)],
+                        buf[piece_of(k, side), block(n)],
+                        preferred_element_type=jnp.float32,
+                    )
+                    for k in range(2)
+                )
+            acc_ref[:, block(n)] += total
             return carry
 
         lax.fori_loop(0, fold, one, 0)
 
-    def turned(l, a):
+    def turned(l, a, side=None):
         base = spot(l, a, 0)
 
         def one(n, carry):
-            total = jnp.zeros((rows, rows), jnp.float32)
+            total = 0.0
             for k in range(0, fold, 2):
                 left = pl.ds(pl.multiple_of((away + k) * rows, rows), 2 * rows)
                 total = total + lax.dot_general(
                     m_ref[:, left],
-                    buf[block(n), pl.ds(k * rows, 2 * rows)],
+                    buf[piece_of(n, side), pl.ds(k * rows, 2 * rows)],
                     (((1,), (1,)), ((), ())),
                     preferred_element_type=jnp.float32,
                 )
-            acc_ref[:, block(base + n)] += total
+            acc_ref[:, piece_of(base + n, side)] += total
             return carry
 
         lax.fori_loop(0, 2, one, 0)
 
-    def mirrored(l, a):
+    def mirrored(l, a, side=None):
         base = spot(l, a, 0)
 
         def lane(k, carry):
@@ -631,14 +661,14 @@
 
             def one(d, inner):
                 s = lax.rem(t + d, fold)
-                tile = buf[block(k), block(d)]
+                tile = buf[piece_of(k, side), block(d)]
                 acc_ref[:, block(s)] += jnp.dot(
-                    m_ref[:, block(near + t)], tile, preferred_element_type=jnp.float32
+                    m_ref[:, piece_of(near + t, side)], tile, preferred_element_type=jnp.float32
                 )
 
                 @pl.when(d > 0)
                 def _():
-                    acc_ref[:, block(t)] += lax.dot_general(
+                    acc_ref[:, piece_of(t, side)] += lax.dot_general(
                         m_ref[:, block(near + s)],
                         tile,
                         (((1,), (1,)), ((), ())),
@@ -787,7 +817,7 @@
         a_far, b_far = spot(front, 1 - x, core), spot(back, 1 - x, core)
 
         def inward(t, q):
-            arrive(*R, t, q)
+            arrive(*R, t, q, 0)
             send("x", *R, t, q)
             send("z", *R, t, q, None, mid)
             send("c", *R, t, q)
@@ -1012,8 +1042,8 @@
     exchange(1, True)
     squares, spread = gather_sums(1)
     stats_ref[0] = theta
-    stats_ref[1] = squares / total
-    stats_ref[2] = spread / total
+    stats_ref[1] = jnp.max(jnp.sqrt(jnp.full((8, 128), squares / total, jnp.float32)))
+    scale_ref[0] = jnp.max(lax.rsqrt(jnp.full((8, 128), spread / total + 1e-06, jnp.float32)))
 
     exchange(0, False)
     exchange(1, False)
@@ -1052,16 +1082,18 @@
     anywhere = pl.BlockSpec(memory_space=pl.ANY)
     vmem = pl.BlockSpec(memory_space=pltpu.VMEM)
     dma = pltpu.SemaphoreType.DMA
-    update, _, _, sums = pl.pallas_call(
+    smem = pl.BlockSpec(memory_space=pltpu.SMEM)
+    update, _, _, stats, scale = pl.pallas_call(
         functools.partial(step_kernel, float(strings) * float(strings)),
         out_shape=(
             jax.ShapeDtypeStruct((rows, half), jnp.float32),
             jax.ShapeDtypeStruct((fold, rows, half), jnp.bfloat16),
             jax.ShapeDtypeStruct((fold, rows, reach), jnp.bfloat16),
-            jax.ShapeDtypeStruct((3,), jnp.float32),
+            jax.ShapeDtypeStruct((2,), jnp.float32),
+            jax.ShapeDtypeStruct((1,), jnp.float32),
         ),
         in_specs=[anywhere, vmem, anywhere, vmem, vmem, vmem],
-        out_specs=(vmem, anywhere, anywhere, pl.BlockSpec(memory_space=pltpu.SMEM)),
+        out_specs=(vmem, anywhere, anywhere, smem, smem),
         scratch_shapes=[
             pltpu.VMEM((rows, half), jnp.float32),
             pltpu.VMEM((rows, strings), jnp.bfloat16),
@@ -1075,9 +1107,9 @@
             pltpu.VMEM((2, 16, 128), jnp.float32),
             pltpu.VMEM((2, count, 16, 128), jnp.float32),
             dma((4,)),
-            dma((80,)),
-            dma((fold, 4)),
-            dma((fold, 4)),
+            dma((100,)),
+            dma((fold, 4, 2)),
+            dma((fold, 4, 2)),
             dma((fold, 2)),
             dma((fold, 2)),
             dma((fold,)),
@@ -1094,7 +1126,7 @@
         ),
         name="whole_step",
     )(ham, tile_mask, coeff, occupation, orbital_energy[None, :], coulomb)
-    return update, sums
+    return update * scale[0], stats
 
 
 CHUNKS = 2
@@ -1106,7 +1138,7 @@
     fold = tile_cols // tile_rows
     direct = lax.axis_size("col") == 2 and lax.axis_size("row") == 16
     if direct:
-        result = whole_step(ham, tile_mask, coeff, occupation, orbital_energy, coulomb)
+        return whole_step(ham, tile_mask, coeff, occupation, orbital_energy, coulomb)
     else:
         occ_float = occupation.astype(jnp.float32)
         occ_alpha = lax.dynamic_slice_in_dim(occ_float, lax.axis_index("row") * tile_rows, tile_rows, 1)

time: 378 us -> 370 us (0.979)
  Pallas kernels: 365 us -> 360 us
    pallas_call x1, Pallas kernels: 365 us -> 360 us  [whole_step(): pl.pallas_call(functools.partial(step_kernel, float(strings) * float(stri...]
where the time goes in v6:
time: 370 us; the launch traced here: 369 us
  Pallas kernels  360 us (97%)
  other arithmetic  8.42 us (2%)
    pallas_call x1, Pallas kernels, whole_step(): pl.pallas_call(functools.partial(step_kernel, float(strings) * float(stri...  360 us
    mul x1, other arithmetic, whole_step(): return (update * scale[0], stats)  8.42 us

profile of v6, /device:TPU:0, one launch (start us, length us, event | category | flops | bytes accessed | tf_op | source)
XLA Modules:
  0.0 369.4 jit_solution(14797859113678737266)
XLA Ops:
  0.6 359.8 %whole_step.1 = (f32[512,4096]{1,0:T(8,128)}, bf16[8,512,4096]{2,1,0:T(8,128)(2,1)}, bf16[8,512,2560]{2,1,0:T(8,128)(2,1)}, f32[2]{0:T(128)}, f32[1]{0:T(128)}) custom-call(bf16[512,8192]{1,0:T(8,128)(2,1)} %ham_ref.1, s32[16,256]{1,0:T(8,128)} %mask_ref.1, bf16[512,4096]{1,0:T(8,128)(2,1)} %coeff_ref.1, s32[16,8192]{1,0:T(8,128)} %occ_ref.1, ...), custom_call_target="tpu_custom_call" | custom-call | tf_op jit(solution)/shard_map/whole_step/pallas_call | solution.py:1086
  360.4 0.0 copy-start
  360.4 8.4 %broadcast_multiply_fusion = f32[512,4096]{1,0:T(8,128)} fusion(f32[512,4096]{1,0:T(8,128)} %get-tuple-element.5, f32[]{:T(128)} %bitcast.1), kind=kLoop, calls=%fused_computation | loop fusion | flops 2097152 | bytes 16777220 | tf_op jit(solution)/shard_map/mul | solution.py:1129
  368.8 0.0 copy-done
  368.8 0.5 copy.9
Async XLA Ops:
  360.4 8.4 %copy-start = (f32[2]{0:T(128)S(1)}, f32[2]{0:T(128)}, u32[]{:S(2)}) copy-start(f32[2]{0:T(128)} %get-tuple-element.11) | copy-start | bytes 28
